TPU v7x, 128 devices: a whole 4x4x4 slice. The times are simulated.
128 devices in a mesh: curve: 16 (over z, y), sub: 8 (over x, core).
Axes of the slice: x: 4, y: 4, z: 4, core: 2. Of those that a mesh axis runs over, the one named last changes fastest.
Arguments:
- coarse: float32 [1024, 6, 16, 256], P(('curve', 'sub')), may hold values from -6 to 6
- tags: int32 [1024], P(('curve', 'sub')), may hold values from 0 to 1, as said below
- box_x: int32 [1024], P(('curve', 'sub')), may hold values from 2 to 2049, as said below
- new_counts: int32 [128], P(('curve', 'sub')), may hold values from 1 to 8, as said below
- courant: float32 [6], replicated, may hold values from 0.3 to 0.9
Outputs:
- fine_state: float32 [1024, 6, 32, 1024], P(('curve', 'sub'))
Inputs may be any that keep to these rules, and one draw needn't show every extreme that they name: `tags`: each device refines 2 to 8 of its boxes, the first device 1 + 2 or more. `box_x`: along the curve order the refined boxes' values rise strictly; the refined box with id new_start[p] is the right neighbour of the one before it for every device p after the first; boxes that are not refined hold 2049. `new_counts`: they sum to the number of refined boxes; every fine box is owned by the device that holds its coarse box or by a device next to it in curve order; between two such devices at most 2 boxes pass in one direction, and a device keeps at least one of its own; the first device passes exactly 2 boxes to the second.
All inputs are finite; a program needn't handle non-finite values.
Results may differ from a plain program's by a relative error of at most 0.0003.
Values sent between devices are 32-bit elements; how exact they have to be, the bound alone decides.
A program may use at most 64 MiB of HBM per device.

v0:
```python
import jax
import jax.numpy as jnp
from jax import lax
from jax.sharding import PartitionSpec as P

MOVE = 2


def passed_along(value, axis, steps):
    count = lax.axis_size(axis)
    initial, last = (max(0, -steps), min(count, count - steps))
    return lax.ppermute(value, axis, [(source, source + steps) for source in range(initial, last)])


def carried_in(part, axis, combine, identity):
    place = lax.axis_index(axis)
    gathered = jax.tree.map(lambda a: lax.all_gather(a, axis), part)
    state = jax.tree.map(lambda a, e: jnp.zeros_like(a) + jnp.asarray(e, a.dtype), part, identity)

    def one(step, state):
        return combine(
            state, jax.tree.map(lambda a: lax.dynamic_index_in_dim(a, step, 0, False), gathered)
        )

    return lax.fori_loop(0, place, one, state)


def prolong_table(coarse_len):
    position = jnp.arange(coarse_len)
    identity = (position[:, None] == position[None, :]).astype(jnp.float32)
    ahead = jnp.concatenate([identity[1:], identity[-1:]], 0)
    behind = jnp.concatenate([identity[:1], identity[:-1]], 0)
    at_edge = (position == 0) | (position == coarse_len - 1)
    divisor = jnp.where(at_edge, 1.0, 2.0).astype(jnp.float32)
    slopes = (ahead - behind) / divisor[:, None]
    fine_pos = jnp.arange(2 * coarse_len)
    signs = jnp.where(fine_pos % 2 == 0, -0.25, 0.25).astype(jnp.float32)
    return jnp.repeat(identity, 2, axis=0) + signs[:, None] * jnp.repeat(slopes, 2, axis=0)


def prolong(coarse_boxes):
    box_count = coarse_boxes.shape[0]
    fields = coarse_boxes.shape[1]
    half_len = coarse_boxes.shape[2]
    line_table = prolong_table(half_len)
    plane_table = jnp.kron(line_table, line_table)
    spread = jnp.dot(
        coarse_boxes.reshape(-1, half_len * half_len),
        plane_table.T,
        precision=lax.Precision.HIGHEST,
    )
    spread = spread.reshape(box_count, fields, half_len, 4 * half_len * half_len)
    return jnp.einsum("fx,bcxy->bcfy", line_table, spread, precision=lax.Precision.HIGHEST)


def ppm_step(extended, courant):
    courant_f = courant[None, :, None, None]
    length = extended.shape[2]
    interface = 7.0 / 12.0 * (
        extended[:, :, 1 : length - 2] + extended[:, :, 2 : length - 1]
    ) - 1.0 / 12.0 * (extended[:, :, 0 : length - 3] + extended[:, :, 3:length])
    left_face = interface[:, :, 0 : length - 4]
    right_face = interface[:, :, 1 : length - 3]
    centre = extended[:, :, 2 : length - 2]
    jump_size = right_face - left_face
    curvature = 6.0 * (centre - 0.5 * (left_face + right_face))
    fluxes = courant_f * (
        right_face - 0.5 * courant_f * (jump_size - (1.0 - 2.0 / 3.0 * courant_f) * curvature)
    )
    return extended[:, :, 3 : length - 2] - (fluxes[:, :, 1:] - fluxes[:, :, :-1])


def border(state, coords, wanted, left_width, next_rim, next_coord):
    slot_count = state.shape[0]
    cells = state.shape[2]
    right_width = next_rim.shape[1]
    last_box = lax.dynamic_index_in_dim(state, wanted - 1, 0, keepdims=False)
    tail_rim = last_box[:, cells - left_width :, :]
    tail_coord = lax.dynamic_slice_in_dim(coords, wanted - 1, 1, 0)
    prev_rim, prev_coord = passed_along((tail_rim, tail_coord), ("curve", "sub"), 1)
    slot_ids = jnp.arange(slot_count)
    left_rim = jnp.concatenate([prev_rim[None], state[:-1, :, cells - left_width :, :]], 0)
    left_coord = jnp.concatenate([prev_coord, coords[:-1]])
    left_adj = left_coord == coords - 1.0
    is_last = slot_ids == wanted - 1
    right_rim = jnp.concatenate([state[1:, :, :right_width, :], next_rim[None]], 0)
    right_rim = jnp.where(is_last[:, None, None, None], next_rim[None], right_rim)
    right_coord = jnp.concatenate([coords[1:], next_coord])
    right_coord = jnp.where(is_last, next_coord[0], right_coord)
    right_adj = right_coord == coords + 1.0
    left_ghost = jnp.where(left_adj[:, None, None, None], left_rim, state[:, :, :1])
    right_ghost = jnp.where(right_adj[:, None, None, None], right_rim, state[:, :, -1:])
    return (jnp.concatenate([left_ghost, state, right_ghost], 2), left_adj, right_adj)


def head_layers(state, coords):
    return passed_along((state[0, :, :2, :], coords[:1]), ("curve", "sub"), -1)


def add_pair(earlier, later):
    return (earlier[0] + later[0], earlier[1] + later[1])


def local(coarse, tags, box_x, new_counts, courant):
    slot_count = coarse.shape[0]
    tagged_count = jnp.sum(tags, keepdims=True)
    zeros_one = jnp.zeros((1,), jnp.int32)
    old_start, new_start = carried_in(
        (tagged_count, new_counts), ("curve", "sub"), add_pair, (zeros_one, zeros_one)
    )
    old_first = old_start[0]
    new_first = new_start[0]
    live_here = tagged_count[0]
    wanted = new_counts[0]
    slot_ids = jnp.arange(slot_count)
    tag_rank = jnp.cumsum(tags) - tags
    selected = (tags[None, :] == 1) & (tag_rank[None, :] == slot_ids[:, None])
    source = jnp.sum(jnp.where(selected, slot_ids[None, :], 0), axis=1)
    packed = jnp.take(coarse, source, axis=0)
    packed_x = jnp.take(box_x, source).astype(jnp.float32)
    payload = prolong(packed)
    move_ids = jnp.arange(MOVE)
    right_pick = jnp.clip(new_first + wanted - old_first + move_ids, 0, slot_count - 1).astype(
        jnp.int32
    )
    from_left, left_x = passed_along(
        (jnp.take(payload, right_pick, axis=0), jnp.take(packed_x, right_pick)), ("curve", "sub"), 1
    )
    head_rank = jnp.clip(new_first - old_first, 0, slot_count - 1).astype(jnp.int32)
    head_from_left = new_first < old_first
    head_box = jnp.where(
        head_from_left,
        from_left[0],
        lax.dynamic_index_in_dim(payload, head_rank, 0, keepdims=False),
    )
    head_coord = jnp.where(
        head_from_left, left_x[:1], lax.dynamic_slice_in_dim(packed_x, head_rank, 1, 0)
    )
    rim_width = 2
    head_rim = head_box[:, :rim_width, :]
    from_right, right_x, next_rim, next_coord = passed_along(
        (payload[:MOVE], packed_x[:MOVE], head_rim, head_coord), ("curve", "sub"), -1
    )
    global_ids = new_first + slot_ids
    own_rank = global_ids - old_first
    anchor = jnp.where(
        global_ids < old_first,
        slot_count + slot_ids,
        jnp.where(own_rank < live_here, own_rank, slot_count + MOVE + own_rank - live_here),
    )
    anchor = jnp.clip(anchor, 0, slot_count + 2 * MOVE - 1).astype(jnp.int32)
    candidates = jnp.concatenate([payload, from_left, from_right], 0)
    arrived = jnp.take(candidates, anchor, axis=0)
    coords = jnp.take(jnp.concatenate([packed_x, left_x, right_x]), anchor)
    state = arrived
    extended, left_adj, right_adj = border(state, coords, wanted, 3, next_rim, next_coord)
    state = ppm_step(extended, courant)
    later_rim, later_coord = head_layers(state, coords)
    extended, left_adj, right_adj = border(state, coords, wanted, 3, later_rim, later_coord)
    state = ppm_step(extended, courant)
    occupied = slot_ids < wanted
    return jnp.where(occupied[:, None, None, None], state, 0.0)


def solution(mesh):
    in_specs = (
        P(("curve", "sub"), None, None, None),
        P(("curve", "sub")),
        P(("curve", "sub")),
        P(("curve", "sub")),
        P(),
    )
    out_specs = P(("curve", "sub"), None, None, None)
    return jax.shard_map(local, mesh=mesh, in_specs=in_specs, out_specs=out_specs, check_vma=False)
```

profile of v0, /device:TPU:126, one launch (start us, length us, event | category | flops | bytes accessed | tf_op | source)
XLA Modules:
  0.0 479.8 jit_solution(11329905340331782572)
XLA Ops:
  0.1 0.7 broadcast_compare_fusion
  0.8 0.8 reduce-window.9
  1.6 1.3 fusion.56
  3.0 1.3 gather_fusion.3
  5.2 2.6 broadcast_multiply_fusion
  7.8 3.7 mul.127
  11.6 2.8 fusion.29
  14.4 8.3 %fusion.37 = f32[8,6,1024,32]{2,3,1,0:T(8,128)S(1)} fusion(f32[8,6,16,1024]{3,2,1,0:T(8,128)S(1)} %fusion.29, f32[32,16]{1,0:T(8,128)S(1)} %multiply_add_fusion), kind=kOutput, calls=%fused_computation.77 | convolution fusion | flops 301989888 | bytes 9439232 | tf_op jit(solution)/shard_map/fx,bcxy->bcfy/dot_general | solution.py:53
  22.7 2.7 copy-done.3
  25.4 1.3 slice.184
  26.7 2.2 collective-permute-start.1
  29.6 0.7 dynamic-update-slice
  30.3 75.7 %all-reduce.2 = (s32[128]{0:T(128)S(1)}, s32[128]{0:T(128)S(1)}) all-reduce(s32[128]{0:T(128)S(1)} %dynamic-update-slice, s32[128]{0:T(128)S(1)} %dynamic-update-slice.1), channel_id=1, replica_groups=mesh['curve'=16,'sub'=8] {'curve','sub'}, use_global_device_ids=true, to_apply=%add | all-reduce | flops 256 | bytes 2048
  106.0 240.4 %while.12 = (s32[]{:T(128)}, s32[1]{0:T(128)}, s32[1]{0:T(128)}, s32[]{:T(128)}, s32[128,1]{0,1:T(1,128)S(1)}, /*index=5*/s32[128,1]{0,1:T(1,128)S(1)}, s32[]{:T(128)}, s32[]{:T(128)}, s32[]{:T(128)}) while((s32[]{:T(128)}, s32[1]{0:T(128)}, s32[1]{0:T(128)}, s32[]{:T(128)}, s32[128,1]{0,1:T(1,128)S(1)}, /*index=5*/s32[128,1]{0,1:T(1,128)S(1)}, ...), condition=%wide.region_2.3_spmd, body=%wide.region_1.2_spmd.sunk | while | flops 7 | bytes 179 | solution.py:25
  346.4 3.4 gather_fusion.1
  349.9 1.4 broadcast_select_fusion.1
  351.3 3.6 collective-permute-start
  355.5 1.9 collective-permute-start.2
  357.5 3.6 collective-permute-start.3
  362.4 10.9 %collective-permute-done.2 = f32[2]{0:T(128)S(1)} collective-permute-done((f32[2]{0:T(128)S(1)}, f32[2]{0:T(128)S(1)}, u32[]{:S(2)}, u32[]{:S(2)}) %collective-permute-start.2) | collective-permute-done | bytes 40 | tf_op jit(solution)/shard_map/ppermute | solution.py:12
  373.9 3.2 collective-permute-start.6
  377.2 0.6 gather_fusion.5
  378.4 0.7 fusion.54
  379.1 1.9 collective-permute-start.9
  381.0 3.0 collective-permute-start.4
  384.1 2.1 collective-permute-done.4
  386.2 3.3 fusion.48
  389.6 8.0 %pad_maximum_fusion = f32[12,6,32,1024]{3,2,1,0:T(8,128)} fusion(f32[2,6,32,1024]{3,2,1,0:T(8,128)} %collective-permute-done.1, f32[2,6,32,1024]{3,2,1,0:T(8,128)S(1)} %collective-permute-done, f32[8,6,32,1024]{3,2,1,0:T(8,128)} %bitcast.77), kind=kLoop, calls=%fused_computation.12 | loop fusion | flops 4718592 | bytes 18874368 | tf_op jit(solution)/shard_map/concatenate | solution.py:152
  397.6 7.3 %gather_fusion.2 = f32[8,6,32,1024]{3,2,1,0:T(8,128)} fusion(f32[12,6,32,1024]{3,2,1,0:T(8,128)} %pad_maximum_fusion, s32[1024]{0:T(1024)S(1)} %pad_clamp_fusion), kind=kCustom, calls=%fused_computation.2 | custom fusion | bytes 12582944 | tf_op jit(solution)/shard_map/jit(_take)/gather | solution.py:153
  404.9 3.6 broadcast_select_fusion
  409.3 1.3 fusion.31
  410.6 1.9 collective-permute-start.7
  412.6 2.4 collective-permute-start.5
  415.4 3.1 collective-permute-done.5
  418.8 3.8 fusion.10
  422.6 5.7 %fusion.25 = f32[8,6,33,1024]{3,2,1,0:T(8,128)} fusion(f32[8,6,32,1024]{3,2,1,0:T(8,128)S(1)} %broadcast_select_fusion, f32[8,6,3,1024]{3,2,1,0:T(4,128)S(1)} %maximum_select_fusion, f32[8,6,34,1024]{3,2,1,0:T(8,128)S(1)} %fusion.10, f32[6]{0:T(128)S(1)} %get-tuple-element.75, f32[6]{0:T(128)S(1)} %get-tuple-element.74, f32[6]{0:T(128)S(1)} %copy-done.4), kind=kLoop, calls=%fused_computation.46 | loop fusion | flops 16220160 | bytes 26345544 | tf_op jit(solution)/shard_map/mul | solution.py:67
  428.3 12.9 %fusion.28 = f32[8,6,32,1024]{3,2,1,0:T(8,128)} fusion(f32[8,6,33,1024]{3,2,1,0:T(8,128)} %fusion.25, f32[8,6,32,1024]{3,2,1,0:T(8,128)} %gather_fusion.2, pred[8]{0:T(512)(128)(4,1)S(1)} %get-tuple-element.56), kind=kLoop, calls=%fused_computation.53 | loop fusion | flops 4718592 | bytes 25165832 | tf_op jit(solution)/shard_map/sub | solution.py:70
  441.2 1.1 slice_bitcast_fusion
  442.3 2.5 fusion.50
  444.8 1.9 collective-permute-start.10
  446.7 1.2 dynamic-slice_bitcast_fusion
  447.9 1.4 slice.206
  449.4 1.5 slice.201
  451.1 2.6 collective-permute-start.8
  454.1 3.0 collective-permute-done.8
  457.4 3.8 fusion.3
  461.2 5.7 %fusion.19 = f32[8,6,33,1024]{3,2,1,0:T(8,128)} fusion(f32[8,6,32,1024]{3,2,1,0:T(8,128)S(1)} %copy-done.2, f32[8,6,3,1024]{3,2,1,0:T(4,128)S(1)} %maximum_select_fusion.1, f32[8,6,34,1024]{3,2,1,0:T(8,128)S(1)} %fusion.3, f32[6]{0:T(128)S(1)} %get-tuple-element.75, f32[6]{0:T(128)S(1)} %get-tuple-element.74, f32[6]{0:T(128)S(1)} %copy-done.4), kind=kLoop, calls=%fused_computation.37 | loop fusion | flops 16220160 | bytes 26345544 | tf_op jit(solution)/shard_map/mul | solution.py:67
  466.9 12.9 %fusion.27 = f32[8,6,32,1024]{3,2,1,0:T(8,128)} fusion(f32[8,6,32,1024]{3,2,1,0:T(8,128)} %fusion.28, f32[8,6,33,1024]{3,2,1,0:T(8,128)} %fusion.19, pred[8]{0:T(512)(128)(4,1)S(1)} %iota_compare_fusion.3), kind=kLoop, calls=%fused_computation.51 | loop fusion | flops 4718592 | bytes 25165832 | tf_op jit(solution)/shard_map/jit(_where)/select_n | solution.py:162
  (188 shorter events, 86.8 us)
Async XLA Ops:
  0.0 4.6 copy-start
  14.4 348.0 %copy-start.4 = (f32[6]{0:T(128)S(1)}, f32[6]{0:T(128)}, u32[]{:S(2)}) copy-start(f32[6]{0:T(128)} %param.11) | copy-start | bytes 76
  22.7 2.7 copy-start.3
  26.7 362.9 %collective-permute-start.1 = (f32[2,6,32,1024]{3,2,1,0:T(8,128)}, f32[2,6,32,1024]{3,2,1,0:T(8,128)}, u32[]{:S(2)}, u32[]{:S(2)}) collective-permute-start(f32[2,6,32,1024]{3,2,1,0:T(8,128)} %slice.184), channel_id=1, source_target_pairs={{1,0},{2,1},{3,2},{4,3},{5,4},{6,5},{7,6},{8,7},{9,8},{10,9},{11,1... | collective-permute-start | bytes 4718600 | tf_op jit(solution)/shard_map/ppermute | solution.py:12
  351.3 38.3 %collective-permute-start = (f32[2,6,32,1024]{3,2,1,0:T(8,128)}, f32[2,6,32,1024]{3,2,1,0:T(8,128)S(1)}, u32[]{:S(2)}, u32[]{:S(2)}) collective-permute-start(f32[2,6,32,1024]{3,2,1,0:T(8,128)} %broadcast_select_fusion.1), channel_id=1, source_target_pairs={{0,1},{1,2},{2,3},{3,4},{4,5},{5,6},{6,7},{7,8},{8,9},{9,10},{10,1... | collective-permute-start | bytes 4718600 | tf_op jit(solution)/shard_map/ppermute | solution.py:12
  355.5 17.7 %collective-permute-start.2 = (f32[2]{0:T(128)S(1)}, f32[2]{0:T(128)S(1)}, u32[]{:S(2)}, u32[]{:S(2)}) collective-permute-start(f32[2]{0:T(128)S(1)} %broadcast_select_fusion.3), channel_id=1, source_target_pairs={{0,1},{1,2},{2,3},{3,4},{4,5},{5,6},{6,7},{7,8},{8,9},{9,10},{10,1... | collective-permute-start | bytes 32 | tf_op jit(solution)/shard_map/ppermute | solution.py:12
  357.5 19.7 %collective-permute-start.3 = (f32[2]{0:T(128)S(1)}, f32[2]{0:T(128)S(1)}, u32[]{:S(2)}, u32[]{:S(2)}) collective-permute-start(f32[2]{0:T(128)S(1)} %bitcast.74), channel_id=1, source_target_pairs={{1,0},{2,1},{3,2},{4,3},{5,4},{6,5},{7,6},{8,7},{9,8},{10,9},{11,1... | collective-permute-start | bytes 32 | tf_op jit(solution)/shard_map/ppermute | solution.py:12
  373.9 10.2 %collective-permute-start.6 = (f32[1]{0:T(128)}, f32[1]{0:T(128)}, u32[]{:S(2)}, u32[]{:S(2)}) collective-permute-start(f32[1]{0:T(128)} %select_n.278), channel_id=1, source_target_pairs={{1,0},{2,1},{3,2},{4,3},{5,4},{6,5},{7,6},{8,7},{9,8},{10,9},{11,1... | collective-permute-start | bytes 20 | tf_op jit(solution)/shard_map/ppermute | solution.py:12
  379.1 5.0 %collective-permute-start.9 = (f32[1]{0:T(128)}, f32[1]{0:T(128)}, u32[]{:S(2)}, u32[]{:S(2)}) collective-permute-start(f32[1]{0:T(128)} %get-tuple-element.72), channel_id=1, source_target_pairs={{1,0},{2,1},{3,2},{4,3},{5,4},{6,5},{7,6},{8,7},{9,8},{10,9},{11,1... | collective-permute-start | bytes 20 | tf_op jit(solution)/shard_map/ppermute | solution.py:12
  381.0 5.2 %collective-permute-start.4 = (f32[1]{0:T(128)}, f32[1]{0:T(128)}, u32[]{:S(2)}, u32[]{:S(2)}) collective-permute-start(f32[1]{0:T(128)} %get-tuple-element.73), channel_id=1, source_target_pairs={{0,1},{1,2},{2,3},{3,4},{4,5},{5,6},{6,7},{7,8},{8,9},{9,10},{10,1... | collective-permute-start | bytes 20 | tf_op jit(solution)/shard_map/ppermute | solution.py:12
  410.6 4.5 collective-permute-start.7
  412.6 5.9 %collective-permute-start.5 = (f32[6,3,1024]{2,1,0:T(4,128)S(1)}, f32[6,3,1024]{2,1,0:T(4,128)S(1)}, u32[]{:S(2)}, u32[]{:S(2)}) collective-permute-start(f32[6,3,1024]{2,1,0:T(4,128)S(1)} %slice.185), channel_id=1, source_target_pairs={{0,1},{1,2},{2,3},{3,4},{4,5},{5,6},{6,7},{7,8},{8,9},{9,10},{10,1... | collective-permute-start | bytes 221192 | tf_op jit(solution)/shard_map/ppermute | solution.py:12
  441.2 16.1 %copy-start.2 = (f32[8,6,32,1024]{3,2,1,0:T(8,128)S(1)}, f32[8,6,32,1024]{3,2,1,0:T(8,128)}, u32[]{:S(2)}) copy-start(f32[8,6,32,1024]{3,2,1,0:T(8,128)} %fusion.28) | copy-start | bytes 18874372
  444.8 8.9 %collective-permute-start.10 = (f32[6,2,1024]{2,1,0:T(2,128)S(1)}, f32[6,2,1024]{2,1,0:T(2,128)S(1)}, u32[]{:S(2)}, u32[]{:S(2)}) collective-permute-start(f32[6,2,1024]{2,1,0:T(2,128)S(1)} %slice_bitcast_fusion), channel_id=1, source_target_pairs={{1,0},{2,1},{3,2},{4,3},{5,4},{6,5},{7,6},{8,7},{9,8},{10,9},{11,1... | collective-permute-start | bytes 147464 | tf_op jit(solution)/shard_map/ppermute | solution.py:12
  451.1 5.9 %collective-permute-start.8 = (f32[6,3,1024]{2,1,0:T(4,128)S(1)}, f32[6,3,1024]{2,1,0:T(4,128)S(1)}, u32[]{:S(2)}, u32[]{:S(2)}) collective-permute-start(f32[6,3,1024]{2,1,0:T(4,128)S(1)} %slice.200), channel_id=1, source_target_pairs={{0,1},{1,2},{2,3},{3,4},{4,5},{5,6},{6,7},{7,8},{8,9},{9,10},{10,1... | collective-permute-start | bytes 221192 | tf_op jit(solution)/shard_map/ppermute | solution.py:12
  461.2 18.7 %copy-start.1 = (f32[8,6,16,256]{3,2,1,0:T(8,128)S(1)}, f32[8,6,16,256]{3,2,1,0:T(8,128)}, u32[]{:S(2)}) copy-start(f32[8,6,16,256]{3,2,1,0:T(8,128)} %param.7) | copy-start | bytes 2359300
where the time goes:
time: 485 us; the launch traced here: 480 us
  loops' own time  160 us (33%)
  local copies, waits for them, and re-layouts  113 us (23%)
  blocking collectives  75.7 us (16%)
  other arithmetic  70.8 us (15%)
  starting transfers between devices  28.3 us (6%)
  waiting for transfers between devices  19.1 us (4%)
  matrix products  11.1 us (2%)
    another operation x1, loops' own time, carried_in(): return lax.fori_loop(0, place, one, state)  160 us
    dynamic_slice x126, local copies, waits for them, and re-layouts, one(): lax.dynamic_index_in_dim(a, step, 0, False)  80.7 us
    unnamed x1, blocking collectives  75.7 us
    ppermute x11, starting transfers between devices, passed_along(): lax.ppermute(value, axis, [(source, source + steps) for source in range(i...  28.3 us
    ppermute x11, waiting for transfers between devices, passed_along(): lax.ppermute(value, axis, [(source, source + steps) for source in range(i...  19.1 us
    select_n x1, other arithmetic, local(): return jnp.where(occupied[:, None, None, None], state, 0.0)  12.9 us
    sub x1, other arithmetic, ppm_step(): return extended[:, :, 3:length - 2] - (fluxes[:, :, 1:] - fluxes[:, :, :-1])  12.9 us
    mul x2, other arithmetic, ppm_step(): courant_f * (right_face - 0.5 * courant_f * (jump_size - (1.0 - 2.0 / 3.0...  11.4 us
  transfers between devices with their start and end apart: 11, of which 4 were waited for; matrix products, arithmetic and copies ran while one was open for 21% of the time, Pallas kernels for 0%

commit v1 on v0

v1 whole, which is shorter than its diff:
```python
import functools

import jax
import jax.numpy as jnp
import numpy as np
from jax import lax
from jax.experimental import pallas as pl
from jax.experimental.pallas import tpu as pltpu
from jax.sharding import PartitionSpec as P

MESH = pl.DeviceIdType.MESH
LEFT_REACH, RIGHT_REACH = 3, 2


def line_table(coarse_len):
    table = np.zeros((2 * coarse_len, coarse_len), np.float64)
    for cell in range(2 * coarse_len):
        i, sign = cell // 2, (-0.25 if cell % 2 == 0 else 0.25)
        ahead, behind = min(i + 1, coarse_len - 1), max(i - 1, 0)
        table[cell, i] += 1.0
        table[cell, ahead] += sign / (ahead - behind)
        table[cell, behind] -= sign / (ahead - behind)
    return table


def x_tables(half):
    line = line_table(half)
    fine = 2 * half
    wide = np.zeros((3 * fine, 3 * half))
    for box in range(3):
        wide[box * fine : (box + 1) * fine, box * half : (box + 1) * half] = line
    cols = slice(half - 8, 2 * half + 8)
    joined = wide[fine - 2 * LEFT_REACH : 2 * fine + 2 * RIGHT_REACH, cols]
    alone = np.concatenate(
        [wide[fine : fine + 1]] * LEFT_REACH + [wide[fine : 2 * fine]] + [wide[2 * fine - 1 : 2 * fine]] * RIGHT_REACH
    )[:, cols]
    grow = lambda a, rows: np.tile(np.pad(a, ((0, rows - a.shape[0]), (0, 0))), (1, 4)).astype(np.float32)
    return grow(joined, 48), grow(alone, 40)


def step_taps(c):
    c2 = c * c
    c3 = c2 * c
    right, left, own = c - 2.0 * c2 + c3, c3 - c2, 3.0 * c2 - 2.0 * c3
    t = 1.0 / 12.0
    flux = (
        -t * left,
        7.0 * t * left - t * right,
        7.0 * t * (left + right) + own,
        7.0 * t * right - t * left,
        -t * right,
    )
    return (
        flux[0],
        flux[1] - flux[0],
        flux[2] - flux[1],
        1.0 + flux[3] - flux[2],
        flux[4] - flux[3],
        -flux[4],
    )


def split_pair(mat):
    high = mat.astype(jnp.bfloat16)
    low = (mat - high.astype(jnp.float32)).astype(jnp.bfloat16)
    lane = lax.broadcasted_iota(jnp.int32, mat.shape, 1)
    return jnp.where(lane < 64, high.astype(jnp.float32), low.astype(jnp.float32)).astype(jnp.bfloat16)


def exchange(
    n_curve, n_sub,
    tags, box_x, counts, courant, coarse, joined, alone,
    info, from_left, from_right, from_second, mats,
    held, to_right, to_left, to_second, rows, side, first_step,
    load_sem, box_send, box_recv, side_send, side_recv, sub_send, sub_recv, curve_send, curve_recv,
):
    boxes = coarse.shape[0]
    fields = coarse.shape[1]
    fine = 32
    n_half = n_curve // 2
    curve, sub = lax.axis_index("curve"), lax.axis_index("sub")
    me = curve * n_sub + sub
    total = n_curve * n_sub
    upper = curve // n_half
    place = curve % n_half
    after, before = (me + 1) % total, (me + total - 1) % total
    second = (me + 2) % total
    after_id, before_id = (after // n_sub, after % n_sub), (before // n_sub, before % n_sub)
    second_id = (second // n_sub, second % n_sub)
    back = (me + total - 2) % total
    back_id = (back // n_sub, back % n_sub)
    sub_ids = [(curve, (sub + o) % n_sub) for o in range(1, n_sub)]
    curve_ids = [(upper * n_half + (place + o) % n_half, sub) for o in range(1, n_half)]

    barrier = pltpu.get_barrier_semaphore()
    peers = curve_ids + sub_ids + [after_id, before_id, second_id, back_id]
    for peer in peers:
        pl.semaphore_signal(barrier, inc=1, device_id=peer, device_id_type=MESH)
    load = pltpu.make_async_copy(coarse, held, load_sem)
    load.start()

    rank_box = [jnp.int32(0)] * boxes
    seen = jnp.int32(0)
    for b in range(boxes):
        on = tags[b] == 1
        for r in range(b + 1):
            rank_box[r] = jnp.where(on & (seen == r), b, rank_box[r])
        seen = seen + jnp.where(on, 1, 0)
    live = seen

    def box_of(rank):
        found = jnp.int32(0)
        for r in range(boxes):
            found = jnp.where(rank == r, rank_box[r], found)
        return found

    tail_box = [box_of(live - 3 + k) for k in range(3)]
    head_box = [rank_box[k] for k in range(3)]
    lane = lax.broadcasted_iota(jnp.int32, (1, 128), 1)
    row = jnp.where(lane == 0, counts[0] - live, jnp.where(lane == 7, live, 0))
    for k in range(3):
        row = jnp.where(lane == 1 + k, box_x[tail_box[k]], row)
        row = jnp.where(lane == 4 + k, box_x[head_box[k]], row)
    rows[place, sub] = row

    load.wait()
    for f in range(fields):
        at, rim, low = 32 * f, 32 * fields + 8 * (f // 2), 4 * (f % 2)
        to_right[at : at + 16, :] = held[tail_box[1], f]
        to_right[at + 16 : at + 32, :] = held[tail_box[2], f]
        to_right[rim + low : rim + low + 4, :] = held[tail_box[0], f, 12:16, :]
        to_second[rim - 32 * fields + low : rim - 32 * fields + low + 4, :] = held[tail_box[2], f, 12:16, :]
        to_left[at : at + 16, :] = held[head_box[0], f]
        to_left[at + 16 : at + 32, :] = held[head_box[1], f]
        to_left[rim + low : rim + low + 4, :] = held[head_box[2], f, 0:4, :]
    pl.semaphore_wait(barrier, len(peers))

    def send(src, dst, send_sem, recv_sem, peer):
        copy = pltpu.make_async_remote_copy(
            src_ref=src, dst_ref=dst, send_sem=send_sem, recv_sem=recv_sem, device_id=peer, device_id_type=MESH
        )
        copy.start()
        return copy

    mine = rows.at[place, sub]
    sub_copies = [send(mine, mine, sub_send.at[o], sub_recv.at[o], peer) for o, peer in enumerate(sub_ids)]
    side_copies = [
        send(mine, side.at[0], side_send.at[0], side_recv.at[0], after_id),
        send(mine, side.at[1], side_send.at[1], side_recv.at[1], before_id),
        send(mine, side.at[2], side_send.at[2], side_recv.at[2], second_id),
    ]
    box_copies = [
        send(to_right, from_left, box_send.at[0], box_recv.at[0], after_id),
        send(to_left, from_right, box_send.at[1], box_recv.at[1], before_id),
        send(to_second, from_second, box_send.at[2], box_recv.at[2], second_id),
    ]

    for copy in sub_copies:
        copy.wait_recv()
    group = rows.at[place]
    curve_copies = [
        send(group, group, curve_send.at[o], curve_recv.at[o], peer) for o, peer in enumerate(curve_ids)
    ]

    for f in range(fields):
        taps = step_taps(courant[f])
        both = []
        for s in range(11):
            terms = [taps[m] * taps[s - m] for m in range(6) if 0 <= s - m < 6]
            both.append(functools.reduce(lambda a, b: a + b, terms))
        mat = both[0] * joined[0:fine, :]
        for s in range(1, 11):
            mat = mat + both[s] * joined[s : s + fine, :]
        mats[f, 1] = split_pair(mat)
        one = taps[0] * alone[0:fine, :]
        for s in range(1, 6):
            one = one + taps[s] * alone[s : s + fine, :]
        first_step[0:8, :] = jnp.broadcast_to(one[0:1, :], (8, 128))
        first_step[8 : 8 + fine, :] = one
        first_step[8 + fine : 16 + fine, :] = jnp.broadcast_to(one[fine - 1 : fine, :], (8, 128))
        two = taps[0] * first_step[5 : 5 + fine, :]
        for s in range(1, 6):
            two = two + taps[s] * first_step[5 + s : 5 + s + fine, :]
        mats[f, 0] = split_pair(two)
        mats[f, 2] = jnp.zeros((fine, 128), jnp.bfloat16)

    for copy in side_copies:
        copy.wait_recv()
    left_row, right_row, second_row = side[0], side[1], side[2]
    left_x = [jnp.sum(jnp.where(lane == 1 + k, left_row, 0)) for k in range(3)]
    short = jnp.sum(jnp.where(lane == 7, left_row, 0)) < 3
    left_x[0] = jnp.where(short, jnp.sum(jnp.where(lane == 3, second_row, 0)), left_x[0])
    info[12] = jnp.where(short, 1, 0)
    right_x = [jnp.sum(jnp.where(lane == 4 + k, right_row, 0)) for k in range(3)]

    for copy in curve_copies:
        copy.wait_recv()
    shape = rows.shape
    order = lax.broadcasted_iota(jnp.int32, shape, 0) * n_sub + lax.broadcasted_iota(jnp.int32, shape, 1)
    lanes = lax.broadcasted_iota(jnp.int32, shape, 3)
    spot = place * n_sub + sub
    below = jnp.where((lanes == 0) & (order < spot), rows[...], 0)
    above = jnp.where((lanes == 0) & (order >= spot), rows[...], 0)
    offset = jnp.sum(jnp.where(upper == 0, below, -above))

    def coord_of(rank):
        found = left_x[0]
        for k in range(3):
            found = jnp.where(rank == k - 3, left_x[k], found)
        for r in range(boxes):
            found = jnp.where((rank == r) & (rank < live), box_x[rank_box[r]], found)
        for k in range(3):
            found = jnp.where(rank == live + k, right_x[k], found)
        return found

    def start_of(rank):
        inside = 40 + 16 * box_of(rank)
        return jnp.where(rank < 0, 40 + 16 * rank, jnp.where(rank < live, inside, 168 + 16 * (rank - live)))

    ranks = [jnp.clip(offset + j, -3, live + 2) for j in range(-1, boxes + 1)]
    coords = [coord_of(r) for r in ranks]
    for j in range(boxes + 2):
        info[j] = start_of(ranks[j])
    for j in range(boxes):
        rank = ranks[j + 1]
        used = j < counts[0]
        on_left = (coords[j] == coords[j + 1] - 1) & ((me > 0) | (rank > 0))
        on_right = (coords[j + 2] == coords[j + 1] + 1) & ((me < total - 1) | (rank < live - 1))
        info[16 + j] = jnp.where(used, jnp.where(on_left, 1, 0), 2)
        info[24 + j] = jnp.where(used, jnp.where(on_right, 1, 0), 2)

    for copy in box_copies:
        copy.wait_recv()
    for copy in sub_copies + side_copies + box_copies + curve_copies:
        copy.wait_send()


def refine(info, coarse, left_boxes, left_rim, second_rim, right_boxes, right_rim, mats, table, out, line):
    boxes = coarse.shape[0]
    even = pl.program_id(0) % 2 == 0
    rim = jnp.where(info[12] == 1, second_rim[...], left_rim[...])
    line[0:8, :] = jnp.where(even, pltpu.roll(rim, 4, 0), rim)
    line[8:40, :] = left_boxes[...]
    for b in range(boxes):
        line[40 + 16 * b : 56 + 16 * b, :] = coarse[b, 0]
    line[168:200, :] = right_boxes[...]
    rim = right_rim[...]
    rim = jnp.where(even, rim, pltpu.roll(rim, 4, 0))
    line[200:208, :] = rim
    line[208:216, :] = rim
    parts = []
    for j in range(boxes):
        at = pl.multiple_of(info[j + 1], 8)
        left_at = pl.multiple_of(info[j] + 8, 8)
        right_at = pl.multiple_of(info[j + 2], 8)
        data = jnp.concatenate(
            [line[pl.ds(left_at, 8), :], line[pl.ds(at, 16), :], line[pl.ds(right_at, 8), :]], axis=0
        )
        high = data.astype(jnp.bfloat16)
        low = (data - high.astype(jnp.float32)).astype(jnp.bfloat16)
        stacked = jnp.concatenate([high, low, high, low], axis=0)
        mat = jnp.concatenate([mats[0, info[16 + j], 0:16, :], mats[0, info[24 + j], 16:32, :]], axis=0)
        parts.append(jnp.dot(mat, stacked, preferred_element_type=jnp.float32))
    moved = jnp.concatenate(parts, axis=0)
    high = moved.astype(jnp.bfloat16)
    low = (moved - high.astype(jnp.float32)).astype(jnp.bfloat16)
    spread = jnp.dot(high, table[...], preferred_element_type=jnp.float32)
    spread = spread + jnp.dot(low, table[...], preferred_element_type=jnp.float32)
    out[...] = spread.reshape(out.shape)


def local(n_curve, n_sub, coarse, tags, box_x, counts, courant):
    boxes, fields, half, plane = coarse.shape
    fine = 2 * half
    joined, alone = x_tables(half)
    line = line_table(half)
    table = jnp.asarray(np.kron(line, line).T, jnp.bfloat16)
    smem = pl.BlockSpec(memory_space=pltpu.SMEM)
    vmem = pl.BlockSpec(memory_space=pltpu.VMEM)
    anywhere = pl.BlockSpec(memory_space=pl.ANY)
    packed = 32 * fields + 4 * fields
    edge = jax.ShapeDtypeStruct((packed, plane), jnp.float32)
    dma = pltpu.SemaphoreType.DMA
    n_half = n_curve // 2
    info, from_left, from_right, from_second, mats = pl.pallas_call(
        functools.partial(exchange, n_curve, n_sub),
        out_shape=(
            jax.ShapeDtypeStruct((32,), jnp.int32),
            edge,
            edge,
            jax.ShapeDtypeStruct((4 * fields, plane), jnp.float32),
            jax.ShapeDtypeStruct((fields, 3, fine, 128), jnp.bfloat16),
        ),
        in_specs=[smem, smem, smem, smem, anywhere, vmem, vmem],
        out_specs=(smem, anywhere, anywhere, anywhere, vmem),
        scratch_shapes=[
            pltpu.VMEM(coarse.shape, jnp.float32),
            pltpu.VMEM((packed, plane), jnp.float32),
            pltpu.VMEM((packed, plane), jnp.float32),
            pltpu.VMEM((4 * fields, plane), jnp.float32),
            pltpu.VMEM((n_half, n_sub, 1, 128), jnp.int32),
            pltpu.VMEM((3, 1, 128), jnp.int32),
            pltpu.VMEM((48, 128), jnp.float32),
            dma,
            dma((3,)),
            dma((3,)),
            dma((3,)),
            dma((3,)),
            dma((n_sub - 1,)),
            dma((n_sub - 1,)),
            dma((n_half - 1,)),
            dma((n_half - 1,)),
        ],
        compiler_params=pltpu.CompilerParams(collective_id=0, has_side_effects=True),
        name="exchange",
    )(tags, box_x, counts, courant, coarse, jnp.asarray(joined), jnp.asarray(alone))
    return pl.pallas_call(
        refine,
        out_shape=jax.ShapeDtypeStruct((boxes, fields, fine, 4 * plane), jnp.float32),
        grid=(fields,),
        in_specs=[
            smem,
            pl.BlockSpec((boxes, 1, half, plane), lambda f: (0, f, 0, 0)),
            pl.BlockSpec((32, plane), lambda f: (f, 0)),
            pl.BlockSpec((8, plane), lambda f: (4 * fields + f // 2, 0)),
            pl.BlockSpec((8, plane), lambda f: (f // 2, 0)),
            pl.BlockSpec((32, plane), lambda f: (f, 0)),
            pl.BlockSpec((8, plane), lambda f: (4 * fields + f // 2, 0)),
            pl.BlockSpec((1, 3, fine, 128), lambda f: (f, 0, 0, 0)),
            pl.BlockSpec((plane, 4 * plane), lambda f: (0, 0)),
        ],
        out_specs=pl.BlockSpec((boxes, 1, fine, 4 * plane), lambda f: (0, f, 0, 0)),
        scratch_shapes=[pltpu.VMEM((216, plane), jnp.float32)],
        name="refine",
    )(info, coarse, from_left, from_left, from_second, from_right, from_right, mats, table)


def solution(mesh):
    both = ("curve", "sub")
    in_specs = (P(both, None, None, None), P(both), P(both), P(both), P())
    return jax.shard_map(
        functools.partial(local, mesh.shape["curve"], mesh.shape["sub"]),
        mesh=mesh,
        in_specs=in_specs,
        out_specs=P(both, None, None, None),
        check_vma=False,
    )
```

time: 485 us -> 25.3 us (0.05)
  the two profiles are of different devices: /device:TPU:126 before, /device:TPU:1 now
where the time goes in v1:
time: 25.3 us; the launch traced here: 24.9 us
  Pallas kernels  24.3 us (96%)
  between operations  0.66 us (3%)
    pallas_call x1, Pallas kernels, local(): pl.pallas_call(functools.partial(exchange, n_curve, n_sub), out_shape=(ja...  17 us
    pallas_call x1, Pallas kernels, local(): pl.pallas_call(refine, out_shape=jax.ShapeDtypeStruct((boxes, fields, fin...  7.33 us

profile of v1, /device:TPU:1, one launch (start us, length us, event | category | flops | bytes accessed | tf_op | source)
XLA Modules:
  0.0 24.9 jit_solution(16647399478991190545)
XLA Ops:
  0.7 17.0 %exchange.1 = (s32[32]{0:T(128)}, f32[216,256]{1,0:T(8,128)}, f32[216,256]{1,0:T(8,128)}, f32[24,256]{1,0:T(8,128)}, bf16[6,3,32,128]{3,2,1,0:T(8,128)(2,1)}) custom-call(s32[8]{0:T(128)} %tags.1, s32[8]{0:T(128)} %box_x.1, s32[1]{0:T(128)S(6)} %copy.9.counts, f32[6]{0:T(128)} %courant.1, f32[8,6,16,256]{3,2,1,0:T(8,128)} %coarse.3, ...), custom_call_target="tpu_custom_call" | custom-call | tf_op jit(solution)/shard_map/exchange/pallas_call | solution.py:285
  17.6 7.3 %refine.1 = f32[8,6,32,1024]{3,2,1,0:T(8,128)} custom-call(s32[32]{0:T(128)} %get-tuple-element.10.info, f32[8,6,16,256]{3,2,1,0:T(8,128)} %coarse.3, f32[216,256]{1,0:T(8,128)} %get-tuple-element.11.left_boxes.left_rim, f32[216,256]{1,0:T(8,128)} %get-tuple-element.11.left_boxes.left_rim, f32[24,256]{1,0:T(8,128)} %get-tuple-element.12.second_rim, ...), custom_call_target="tpu_custom_call" | custom-call | tf_op jit(solution)/shard_map/refine/pallas_call | solution.py:317

commit v2 on v1

v2 whole, which is shorter than its diff:
```python
import functools

import jax
import jax.numpy as jnp
import numpy as np
from jax import lax
from jax.experimental import pallas as pl
from jax.experimental.pallas import tpu as pltpu
from jax.sharding import PartitionSpec as P

MESH = pl.DeviceIdType.MESH
MOVE = 2
LEFT_REACH, RIGHT_REACH = 3, 2


def line_table(coarse_len):
    table = np.zeros((2 * coarse_len, coarse_len), np.float64)
    for cell in range(2 * coarse_len):
        i, sign = cell // 2, (-0.25 if cell % 2 == 0 else 0.25)
        ahead, behind = min(i + 1, coarse_len - 1), max(i - 1, 0)
        table[cell, i] += 1.0
        table[cell, ahead] += sign / (ahead - behind)
        table[cell, behind] -= sign / (ahead - behind)
    return table


def x_tables(half):
    line = line_table(half)
    fine = 2 * half
    wide = np.zeros((3 * fine, 3 * half))
    for box in range(3):
        wide[box * fine : (box + 1) * fine, box * half : (box + 1) * half] = line
    cols = np.concatenate([2 * half + np.arange(4), half - 4 + np.arange(4), half + np.arange(half)])
    joined = wide[fine - 2 * LEFT_REACH : 2 * fine + 2 * RIGHT_REACH, cols]
    alone = np.concatenate(
        [wide[fine : fine + 1]] * LEFT_REACH + [wide[fine : 2 * fine]] + [wide[2 * fine - 1 : 2 * fine]] * RIGHT_REACH
    )[:, cols]

    def grow(a, rows):
        a = np.tile(np.pad(a, ((0, rows - a.shape[0]), (0, 0))), (1, 4))
        return np.pad(a, ((0, 0), (0, 128 - a.shape[1]))).astype(np.float32)

    return grow(joined, 48), grow(alone, 40)


def plane_tables(half):
    line = line_table(half)
    table = np.kron(line, line).T
    size = half * half
    lane = np.arange(size // 2)
    picks = [lane, np.where(lane < 32, lane + 128, lane), np.where(lane < 96, lane + 128, lane), lane + 128]
    quarters = []
    for n, pick in enumerate(picks):
        columns = table[:, n * size : (n + 1) * size]
        missed = np.delete(columns, pick, axis=0)
        assert not missed.any()
        quarters.append(np.concatenate([columns[pick], columns[pick]]))
    return np.stack(quarters)


def step_taps(c):
    c2 = c * c
    c3 = c2 * c
    right, left, own = c - 2.0 * c2 + c3, c3 - c2, 3.0 * c2 - 2.0 * c3
    t = 1.0 / 12.0
    flux = (
        -t * left,
        7.0 * t * left - t * right,
        7.0 * t * (left + right) + own,
        7.0 * t * right - t * left,
        -t * right,
    )
    return (
        flux[0],
        flux[1] - flux[0],
        flux[2] - flux[1],
        1.0 + flux[3] - flux[2],
        flux[4] - flux[3],
        -flux[4],
    )


def split_pair(mat):
    high = mat.astype(jnp.bfloat16).astype(jnp.float32)
    lane = lax.broadcasted_iota(jnp.int32, mat.shape, 1)
    return jnp.where(lane < 48, high, mat - high).astype(jnp.bfloat16)


def exchange(
    n_curve, n_sub,
    tags_in, box_x_in, counts_in, courant_in, coarse, joined_in, alone_in,
    info_out, all_rows, from_left, from_right, from_second, mats_out,
    tags, box_x, counts, courant, info, joined, alone, mats,
    held, to_right, to_left, to_second, rows, side, first_step,
    load_sem, out_sem, box_send, box_recv, side_send, side_recv, sub_send, sub_recv, curve_send, curve_recv,
):
    boxes = coarse.shape[0]
    fields = coarse.shape[1]
    fine = 32
    n_half = n_curve // 2
    curve, sub = lax.axis_index("curve"), lax.axis_index("sub")
    me = curve * n_sub + sub
    total = n_curve * n_sub
    upper = curve // n_half
    place = curve % n_half

    def device(index):
        return (index // n_sub, index % n_sub)

    sub_ids = [(curve, (sub + o) % n_sub) for o in range(1, n_sub)]
    curve_ids = [(upper * n_half + (place + o) % n_half, sub) for o in range(1, n_half)]
    chain = [(1, me < total - 1, me > 0), (-1, me > 0, me < total - 1), (2, me < total - 2, me > 1)]

    barrier = pltpu.get_barrier_semaphore()

    def signal(peer):
        pl.semaphore_signal(barrier, inc=1, device_id=peer, device_id_type=MESH)

    loads = [
        pltpu.make_async_copy(a, b, load_sem.at[k])
        for k, (a, b) in enumerate(
            [
                (coarse, held), (tags_in, tags), (box_x_in, box_x), (counts_in, counts), (courant_in, courant),
                (joined_in, joined), (alone_in, alone),
            ]
        )
    ]
    for load in loads:
        load.start()
    for peer in curve_ids + sub_ids:
        signal(peer)
    expected = jnp.int32(len(curve_ids) + len(sub_ids))
    for step, sends, gets in chain + [(-2, me > 1, me < total - 2)]:
        @pl.when(sends)
        def _(step=step):
            signal(device(me + step))
        expected = expected + jnp.where(gets, 1, 0)

    for load in loads[1:4]:
        load.wait()
    rank_box = [jnp.int32(0)] * boxes
    seen = jnp.int32(0)
    for b in range(boxes):
        on = tags[b] == 1
        for r in range(b + 1):
            rank_box[r] = jnp.where(on & (seen == r), b, rank_box[r])
        seen = seen + jnp.where(on, 1, 0)
    live = seen

    def box_of(rank):
        found = jnp.int32(0)
        for r in range(boxes):
            found = jnp.where(rank == r, rank_box[r], found)
        return found

    tail_box = [box_of(live - 3 + k) for k in range(3)]
    head_box = [rank_box[k] for k in range(3)]
    lane = lax.broadcasted_iota(jnp.int32, (1, 128), 1)
    row = jnp.where(lane == 0, counts[0] - live, jnp.where(lane == 7, live, 0))
    for k in range(3):
        row = jnp.where(lane == 1 + k, box_x[tail_box[k]], row)
        row = jnp.where(lane == 4 + k, box_x[head_box[k]], row)
    rows[place, sub] = row

    loads[0].wait()
    for f in range(fields):
        at, rim, low = 32 * f, 32 * fields + 8 * (f // 2), 4 * (f % 2)
        to_right[at : at + 16, :] = held[tail_box[1], f]
        to_right[at + 16 : at + 32, :] = held[tail_box[2], f]
        to_right[rim + low : rim + low + 4, :] = held[tail_box[0], f, 12:16, :]
        to_second[rim - 32 * fields + low : rim - 32 * fields + low + 4, :] = held[tail_box[2], f, 12:16, :]
        to_left[at : at + 16, :] = held[head_box[0], f]
        to_left[at + 16 : at + 32, :] = held[head_box[1], f]
        to_left[rim + low : rim + low + 4, :] = held[head_box[2], f, 0:4, :]
    pl.semaphore_wait(barrier, expected)

    def copy_to(src, dst, send_sem, recv_sem, peer):
        return pltpu.make_async_remote_copy(
            src_ref=src, dst_ref=dst, send_sem=send_sem, recv_sem=recv_sem, device_id=peer, device_id_type=MESH
        )

    mine, group = rows.at[place, sub], rows.at[place]
    sub_copies = [copy_to(mine, mine, sub_send.at[o], sub_recv.at[o], peer) for o, peer in enumerate(sub_ids)]
    curve_copies = [
        copy_to(group, all_rows.at[place], curve_send.at[o], curve_recv.at[o], peer)
        for o, peer in enumerate(curve_ids)
    ]
    box_ends = [(to_right, from_left), (to_left, from_right), (to_second, from_second)]
    box_copies = []
    side_copies = []
    for k, (step, sends, gets) in enumerate(chain):
        peer = device(jnp.clip(me + step, 0, total - 1))
        box_copies.append(copy_to(*box_ends[k], box_send.at[k], box_recv.at[k], peer))
        side_copies.append(copy_to(mine, side.at[k], side_send.at[k], side_recv.at[k], peer))
    for copy in sub_copies:
        copy.start()
    for k, (step, sends, gets) in enumerate(chain):
        @pl.when(sends)
        def _(k=k):
            side_copies[k].start()
            box_copies[k].start()

    for copy in sub_copies:
        copy.wait_recv()
    for copy in curve_copies:
        copy.start()
    keep = pltpu.make_async_copy(group, all_rows.at[place], out_sem.at[0])
    keep.start()

    for load in loads[4:]:
        load.wait()
    for f in range(fields):
        taps = step_taps(courant[f])
        both = []
        for s in range(11):
            terms = [taps[m] * taps[s - m] for m in range(6) if 0 <= s - m < 6]
            both.append(functools.reduce(lambda a, b: a + b, terms))
        mat = both[0] * joined[0:fine, :]
        for s in range(1, 11):
            mat = mat + both[s] * joined[s : s + fine, :]
        mats[f, 1] = split_pair(mat)
        one = taps[0] * alone[0:fine, :]
        for s in range(1, 6):
            one = one + taps[s] * alone[s : s + fine, :]
        first_step[0:8, :] = jnp.broadcast_to(one[0:1, :], (8, 128))
        first_step[8 : 8 + fine, :] = one
        first_step[8 + fine : 16 + fine, :] = jnp.broadcast_to(one[fine - 1 : fine, :], (8, 128))
        two = taps[0] * first_step[5 : 5 + fine, :]
        for s in range(1, 6):
            two = two + taps[s] * first_step[5 + s : 5 + s + fine, :]
        mats[f, 0] = split_pair(two)
        mats[f, 2] = jnp.zeros((fine, 128), jnp.bfloat16)
    save_mats = pltpu.make_async_copy(mats, mats_out, out_sem.at[1])
    save_mats.start()

    for k, (step, sends, gets) in enumerate(chain):
        @pl.when(gets)
        def _(k=k):
            side_copies[k].wait_recv()
    right_row, left_row, second_row = side[1], side[0], side[2]
    left_x = [jnp.sum(jnp.where(lane == 1 + k, left_row, 0)) for k in range(3)]
    short = jnp.sum(jnp.where(lane == 7, left_row, 0)) < 3
    left_x[0] = jnp.where(short, jnp.sum(jnp.where(lane == 3, second_row, 0)), left_x[0])
    right_x = [jnp.sum(jnp.where(lane == 4 + k, right_row, 0)) for k in range(3)]
    last = total - 1
    coord_before = jnp.int32(0)
    for k in range(boxes + 2 * MOVE + 2):
        rank = k - 3
        if rank < 0:
            start = jnp.int32(40 + 16 * rank)
            coord = jnp.where(me > 0, left_x[k], -8)
        else:
            past = rank - live
            own_box = rank_box[rank] if rank < boxes else jnp.int32(0)
            start = jnp.where(past < 0, 40 + 16 * own_box, 168 + 16 * jnp.minimum(past, 2))
            beyond = jnp.where(past == 0, right_x[0], jnp.where(past == 1, right_x[1], right_x[2]))
            beyond = jnp.where(me < last, beyond, -8)
            coord = jnp.where(past < 0, box_x[own_box], beyond)
        info[k] = start
        info[16 + k] = jnp.where(coord_before + 1 == coord, 1, 0) if k else 0
        coord_before = coord
    info[14] = jnp.where(short, 1, 0)
    info[15] = counts[0]
    save_info = pltpu.make_async_copy(info, info_out, out_sem.at[2])
    save_info.start()

    save_mats.wait()
    save_info.wait()
    keep.wait()
    for copy in curve_copies:
        copy.wait_recv()
    for k, (step, sends, gets) in enumerate(chain):
        @pl.when(gets)
        def _(k=k):
            box_copies[k].wait_recv()
    for copy in sub_copies + curve_copies:
        copy.wait_send()
    for k, (step, sends, gets) in enumerate(chain):
        @pl.when(sends)
        def _(k=k):
            side_copies[k].wait_send()
            box_copies[k].wait_send()


def refine(
    n_curve, n_sub,
    info, all_rows, coarse, from_left, from_right, from_second, mats_in, tables_in,
    out,
    line, mats, tables, windows, stage, load_sem, out_sem,
):
    boxes, fields = coarse.shape[:2]
    n_half = n_curve // 2
    loads = []

    def load(src, dst):
        copy = pltpu.make_async_copy(src, dst, load_sem.at[len(loads)])
        copy.start()
        loads.append(copy)

    for b in range(boxes):
        load(coarse.at[b], line.at[:, 40 + 16 * b : 56 + 16 * b, :])
    load(mats_in, mats)
    for f in range(fields):
        load(from_left.at[32 * f : 32 * f + 32], line.at[f, 8:40])
        load(from_right.at[32 * f : 32 * f + 32], line.at[f, 168:200])
    edges = slice(32 * fields, 36 * fields)
    load(from_left.at[edges], stage.at[0, 0, 0 : 4 * fields, 0:256])
    load(from_second, stage.at[0, 1, 0 : 4 * fields, 0:256])
    load(from_right.at[edges], stage.at[0, 2, 0 : 4 * fields, 0:256])
    load(tables_in, tables)

    curve, sub = lax.axis_index("curve"), lax.axis_index("sub")
    shape = all_rows.shape
    order = lax.broadcasted_iota(jnp.int32, shape, 0)
    lanes = lax.broadcasted_iota(jnp.int32, shape, 1)
    spot = (curve % n_half) * n_sub + sub
    below = jnp.where((lanes == 0) & (order < spot), all_rows[...], 0)
    above = jnp.where((lanes == 0) & (order >= spot), all_rows[...], 0)
    offset = jnp.sum(jnp.where(curve < n_half, below, -above))
    wanted = info[15]
    starts, left_starts, right_starts, left_on, right_on, left_mat, right_mat = [], [], [], [], [], [], []
    for j in range(boxes):
        at = offset + 3 + j
        used = j < wanted
        starts.append(pl.multiple_of(jnp.where(used, info[at], 40), 8))
        left_starts.append(pl.multiple_of(info[at - 1] + 8, 8))
        right_starts.append(pl.multiple_of(info[at + 1], 8))
        left_on.append(info[16 + at])
        right_on.append(info[17 + at])
        left_mat.append(jnp.where(used, left_on[j], 2))
        right_mat.append(jnp.where(used, right_on[j], 2))

    for copy in loads:
        copy.wait()
    for pair in range(fields // 2):
        cut = slice(8 * pair, 8 * pair + 8)
        left_rim = jnp.where(info[14] == 1, stage[0, 1, cut, 0:256], stage[0, 0, cut, 0:256])
        right_rim = stage[0, 2, cut, 0:256]
        line[2 * pair, 0:8, :] = pltpu.roll(left_rim, 4, 0)
        line[2 * pair + 1, 0:8, :] = left_rim
        line[2 * pair, 200:208, :] = right_rim
        line[2 * pair + 1, 200:208, :] = pltpu.roll(right_rim, 4, 0)

    top = lax.broadcasted_iota(jnp.int32, (8, 256), 0) < 4
    lane = lax.broadcasted_iota(jnp.int32, (32, 128), 1)

    def along_x(f):
        for j in range(boxes):
            left = jnp.where(left_on[j] == 1, line[f, pl.ds(left_starts[j], 8), :], 0.0)
            right = jnp.where(right_on[j] == 1, line[f, pl.ds(right_starts[j], 8), :], 0.0)
            data = jnp.concatenate([jnp.where(top, right, left), line[f, pl.ds(starts[j], 16), :]], axis=0)
            rest = data - data.astype(jnp.bfloat16).astype(jnp.float32)
            stacked = jnp.concatenate([data, rest], axis=0).astype(jnp.bfloat16)
            stacked = jnp.concatenate([stacked, stacked], axis=0)
            mat = jnp.concatenate([mats[f, left_mat[j], 0:16, :], mats[f, right_mat[j], 16:32, :]], axis=0)
            moved = jnp.dot(mat[:, 0:96], stacked, preferred_element_type=jnp.float32)
            a, b = moved[:, 0:128], moved[:, 128:256]
            for n, part in enumerate([a, jnp.where(lane < 32, b, a), jnp.where(lane < 96, b, a), b]):
                high = part.astype(jnp.bfloat16)
                windows[f % 2, n, 32 * j : 32 * j + 32, 0:128] = high
                windows[f % 2, n, 32 * j : 32 * j + 32, 128:256] = (part - high.astype(jnp.float32)).astype(jnp.bfloat16)

    copies = []
    along_x(0)
    for f in range(fields):
        if f + 1 < fields:
            along_x(f + 1)
        for n in range(4):
            spread = jnp.dot(windows[f % 2, n], tables[n], preferred_element_type=jnp.float32)
            stage[f, :, :, 256 * n : 256 * n + 256] = spread.reshape(boxes, 32, 256)
        copy = pltpu.make_async_copy(stage.at[f], out.at[:, f], out_sem.at[f])
        copy.start()
        copies.append(copy)
    for copy in copies:
        copy.wait()


def local(n_curve, n_sub, coarse, tags, box_x, counts, courant):
    boxes, fields, half, plane = coarse.shape
    fine = 2 * half
    joined, alone = x_tables(half)
    tables = jnp.asarray(plane_tables(half), jnp.bfloat16)
    smem = pl.BlockSpec(memory_space=pltpu.SMEM)
    vmem = pl.BlockSpec(memory_space=pltpu.VMEM)
    anywhere = pl.BlockSpec(memory_space=pl.ANY)
    packed = 36 * fields
    edge = jax.ShapeDtypeStruct((packed, plane), jnp.float32)
    dma = pltpu.SemaphoreType.DMA
    n_half = n_curve // 2
    mats_shape = (fields, 3, fine, 128)
    info, all_rows, from_left, from_right, from_second, mats = pl.pallas_call(
        functools.partial(exchange, n_curve, n_sub),
        out_shape=(
            jax.ShapeDtypeStruct((32,), jnp.int32),
            jax.ShapeDtypeStruct((n_half, n_sub, 1, 128), jnp.int32),
            edge,
            edge,
            jax.ShapeDtypeStruct((4 * fields, plane), jnp.float32),
            jax.ShapeDtypeStruct(mats_shape, jnp.bfloat16),
        ),
        in_specs=[anywhere] * 7,
        out_specs=(anywhere,) * 6,
        scratch_shapes=[
            pltpu.SMEM((boxes,), jnp.int32),
            pltpu.SMEM((boxes,), jnp.int32),
            pltpu.SMEM((1,), jnp.int32),
            pltpu.SMEM((fields,), jnp.float32),
            pltpu.SMEM((32,), jnp.int32),
            pltpu.VMEM((48, 128), jnp.float32),
            pltpu.VMEM((40, 128), jnp.float32),
            pltpu.VMEM(mats_shape, jnp.bfloat16),
            pltpu.VMEM(coarse.shape, jnp.float32),
            pltpu.VMEM((packed, plane), jnp.float32),
            pltpu.VMEM((packed, plane), jnp.float32),
            pltpu.VMEM((4 * fields, plane), jnp.float32),
            pltpu.VMEM((n_half, n_sub, 1, 128), jnp.int32),
            pltpu.VMEM((3, 1, 128), jnp.int32),
            pltpu.VMEM((48, 128), jnp.float32),
            dma((7,)),
            dma((3,)),
            dma((3,)),
            dma((3,)),
            dma((3,)),
            dma((3,)),
            dma((n_sub - 1,)),
            dma((n_sub - 1,)),
            dma((n_half - 1,)),
            dma((n_half - 1,)),
        ],
        compiler_params=pltpu.CompilerParams(collective_id=0, has_side_effects=True),
        name="exchange",
    )(tags, box_x, counts, courant, coarse, jnp.asarray(joined), jnp.asarray(alone))
    return pl.pallas_call(
        functools.partial(refine, n_curve, n_sub),
        out_shape=jax.ShapeDtypeStruct((boxes, fields, fine, 4 * plane), jnp.float32),
        in_specs=[smem, vmem] + [anywhere] * 6,
        out_specs=anywhere,
        scratch_shapes=[
            pltpu.VMEM((fields, 216, plane), jnp.float32),
            pltpu.VMEM(mats_shape, jnp.bfloat16),
            pltpu.VMEM(tables.shape, jnp.bfloat16),
            pltpu.VMEM((2, 4, boxes * fine, plane), jnp.bfloat16),
            pltpu.VMEM((fields, boxes, fine, 4 * plane), jnp.float32),
            dma((boxes + 5 + 2 * fields,)),
            dma((fields,)),
        ],
        name="refine",
    )(info, all_rows.reshape(n_half * n_sub, 128), coarse, from_left, from_right, from_second, mats, tables)


def solution(mesh):
    both = ("curve", "sub")
    in_specs = (P(both, None, None, None), P(both), P(both), P(both), P())
    return jax.shard_map(
        functools.partial(local, mesh.shape["curve"], mesh.shape["sub"]),
        mesh=mesh,
        in_specs=in_specs,
        out_specs=P(both, None, None, None),
        check_vma=False,
    )
```

time: 25.3 us -> 20.4 us (0.81)
  Pallas kernels: 24.3 us -> 19.5 us
    pallas_call x1, Pallas kernels: 17 us -> 13.7 us  [local(): pl.pallas_call(functools.partial(exchange, n_curve, n_sub), out_shape=(ja...]
    pallas_call x1, Pallas kernels: 7.33 us -> 5.81 us  [local(): pl.pallas_call(functools.partial(refine, n_curve, n_sub), out_shape=jax.S...]
where the time goes in v2:
time: 20.4 us; the launch traced here: 20.2 us
  Pallas kernels  19.5 us (96%)
  between operations  0.66 us (3%)
    pallas_call x1, Pallas kernels, local(): pl.pallas_call(functools.partial(exchange, n_curve, n_sub), out_shape=(ja...  13.7 us
    pallas_call x1, Pallas kernels, local(): pl.pallas_call(functools.partial(refine, n_curve, n_sub), out_shape=jax.S...  5.81 us

profile of v2, /device:TPU:1, one launch (start us, length us, event | category | flops | bytes accessed | tf_op | source)
XLA Modules:
  0.0 20.2 jit_solution(9817953966605817693)
XLA Ops:
  0.7 13.7 %exchange.1 = (s32[32]{0:T(128)}, s32[8,8,1,128]{3,2,1,0:T(1,128)}, f32[216,256]{1,0:T(8,128)}, f32[216,256]{1,0:T(8,128)}, f32[24,256]{1,0:T(8,128)}, /*index=5*/bf16[6,3,32,128]{3,2,1,0:T(8,128)(2,1)}) custom-call(s32[8]{0:T(128)} %tags_in.1, s32[8]{0:T(128)} %box_x_in.1, s32[1]{0:T(128)S(6)} %copy.9.counts_in, f32[6]{0:T(128)} %courant_in.1, ...), custom_call_target="tpu_custom_call" | custom-call | tf_op jit(solution)/shard_map/exchange/pallas_call | solution.py:391
  14.4 5.8 %refine.1 = f32[8,6,32,1024]{3,2,1,0:T(8,128)} custom-call(s32[32]{0:T(128)} %get-tuple-element.11.info, s32[64,128]{1,0:T(8,128)} %bitcast.1, f32[8,6,16,256]{3,2,1,0:T(8,128)} %coarse.3, f32[216,256]{1,0:T(8,128)} %get-tuple-element.13.from_left, f32[216,256]{1,0:T(8,128)} %get-tuple-element.14.from_right, f32[24,256]{1,0:T(8,128)} %get-tuple-element.15.from_second, ...), custom_call_target="tpu_custom_call" | custom-call | tf_op jit(solution)/shard_map/refine/pallas_call | solution.py:433

commit v3 on v2

v3 whole, which is shorter than its diff:
```python
import functools

import jax
import jax.numpy as jnp
import numpy as np
from jax import lax
from jax.experimental import pallas as pl
from jax.experimental.pallas import tpu as pltpu
from jax.sharding import PartitionSpec as P

MESH = pl.DeviceIdType.MESH
MOVE = 2
LEFT_REACH, RIGHT_REACH = 3, 2


def line_table(coarse_len):
    table = np.zeros((2 * coarse_len, coarse_len), np.float64)
    for cell in range(2 * coarse_len):
        i, sign = cell // 2, (-0.25 if cell % 2 == 0 else 0.25)
        ahead, behind = min(i + 1, coarse_len - 1), max(i - 1, 0)
        table[cell, i] += 1.0
        table[cell, ahead] += sign / (ahead - behind)
        table[cell, behind] -= sign / (ahead - behind)
    return table


def x_tables(half):
    line = line_table(half)
    fine = 2 * half
    wide = np.zeros((3 * fine, 3 * half))
    for box in range(3):
        wide[box * fine : (box + 1) * fine, box * half : (box + 1) * half] = line
    cols = np.concatenate([2 * half + np.arange(4), half - 4 + np.arange(4), half + np.arange(half)])
    joined = wide[fine - 2 * LEFT_REACH : 2 * fine + 2 * RIGHT_REACH, cols]
    alone = np.concatenate(
        [wide[fine : fine + 1]] * LEFT_REACH + [wide[fine : 2 * fine]] + [wide[2 * fine - 1 : 2 * fine]] * RIGHT_REACH
    )[:, cols]

    def grow(a, rows):
        a = np.tile(np.pad(a, ((0, rows - a.shape[0]), (0, 0))), (1, 4))
        return np.pad(a, ((0, 0), (0, 128 - a.shape[1]))).astype(np.float32)

    return grow(joined, 48), grow(alone, 40)


def plane_tables(half):
    line = line_table(half)
    table = np.kron(line, line).T
    size = half * half
    lane = np.arange(size // 2)
    picks = [lane, np.where(lane < 32, lane + 128, lane), np.where(lane < 96, lane + 128, lane), lane + 128]
    quarters = []
    for n, pick in enumerate(picks):
        columns = table[:, n * size : (n + 1) * size]
        missed = np.delete(columns, pick, axis=0)
        assert not missed.any()
        quarters.append(np.concatenate([columns[pick], columns[pick]]))
    return np.stack(quarters)


def step_taps(c):
    c2 = c * c
    c3 = c2 * c
    right, left, own = c - 2.0 * c2 + c3, c3 - c2, 3.0 * c2 - 2.0 * c3
    t = 1.0 / 12.0
    flux = (
        -t * left,
        7.0 * t * left - t * right,
        7.0 * t * (left + right) + own,
        7.0 * t * right - t * left,
        -t * right,
    )
    return (
        flux[0],
        flux[1] - flux[0],
        flux[2] - flux[1],
        1.0 + flux[3] - flux[2],
        flux[4] - flux[3],
        -flux[4],
    )


def split_pair(mat):
    high = mat.astype(jnp.bfloat16).astype(jnp.float32)
    lane = lax.broadcasted_iota(jnp.int32, mat.shape, 1)
    return jnp.where(lane < 48, high, mat - high).astype(jnp.bfloat16)


def exchange(
    n_curve, n_sub,
    tags_in, box_x_in, courant_in, coarse, joined_in, alone_in, tables_in, counts,
    all_rows, cand,
    tags, box_x, courant, joined, alone, tables, mats, windows,
    held, to_right, to_left, to_second, from_left, from_right, from_second, rows, side, first_step,
    load_sem, out_sem, box_send, box_recv, side_send, side_recv, sub_send, sub_recv, curve_send, curve_recv,
):
    boxes = coarse.shape[0]
    fields = coarse.shape[1]
    fine = 32
    n_half = n_curve // 2
    curve, sub = lax.axis_index("curve"), lax.axis_index("sub")
    me = curve * n_sub + sub
    total = n_curve * n_sub
    upper = curve // n_half
    place = curve % n_half

    def device(index):
        return (index // n_sub, index % n_sub)

    sub_ids = [(curve, (sub + o) % n_sub) for o in range(1, n_sub)]
    curve_ids = [(upper * n_half + (place + o) % n_half, sub) for o in range(1, n_half)]
    chain = [(1, me < total - 1, me > 0), (-1, me > 0, me < total - 1), (2, me < total - 2, me > 1)]

    barrier = pltpu.get_barrier_semaphore()

    def signal(peer):
        pl.semaphore_signal(barrier, inc=1, device_id=peer, device_id_type=MESH)

    loads = [
        pltpu.make_async_copy(a, b, load_sem.at[k])
        for k, (a, b) in enumerate(
            [
                (coarse, held), (tags_in, tags), (box_x_in, box_x), (courant_in, courant), (joined_in, joined),
                (alone_in, alone), (tables_in, tables),
            ]
        )
    ]
    for load in loads:
        load.start()
    for peer in curve_ids + sub_ids:
        signal(peer)
    expected = jnp.int32(len(curve_ids) + len(sub_ids))
    for step, sends, gets in chain + [(-2, me > 1, me < total - 2)]:
        @pl.when(sends)
        def _(step=step):
            signal(device(me + step))
        expected = expected + jnp.where(gets, 1, 0)

    for load in loads[1:3]:
        load.wait()
    rank_box = [jnp.int32(0)] * boxes
    seen = jnp.int32(0)
    for b in range(boxes):
        on = tags[b] == 1
        for r in range(b + 1):
            rank_box[r] = jnp.where(on & (seen == r), b, rank_box[r])
        seen = seen + jnp.where(on, 1, 0)
    live = seen

    def box_of(rank):
        found = jnp.int32(0)
        for r in range(boxes):
            found = jnp.where(rank == r, rank_box[r], found)
        return found

    tail_box = [box_of(live - 3 + k) for k in range(3)]
    head_box = [rank_box[k] for k in range(3)]
    lane = lax.broadcasted_iota(jnp.int32, (1, 128), 1)
    row = jnp.where(lane == 0, counts[0] - live, jnp.where(lane == 7, live, 0))
    for k in range(3):
        row = jnp.where(lane == 1 + k, box_x[tail_box[k]], row)
        row = jnp.where(lane == 4 + k, box_x[head_box[k]], row)
    rows[place, sub] = row

    loads[0].wait()
    for f in range(fields):
        at, rim, low = 32 * f, 32 * fields + 8 * (f // 2), 4 * (f % 2)
        to_right[at : at + 16, :] = held[tail_box[1], f]
        to_right[at + 16 : at + 32, :] = held[tail_box[2], f]
        to_right[rim + low : rim + low + 4, :] = held[tail_box[0], f, 12:16, :]
        to_second[rim - 32 * fields + low : rim - 32 * fields + low + 4, :] = held[tail_box[2], f, 12:16, :]
        to_left[at : at + 16, :] = held[head_box[0], f]
        to_left[at + 16 : at + 32, :] = held[head_box[1], f]
        to_left[rim + low : rim + low + 4, :] = held[head_box[2], f, 0:4, :]
    pl.semaphore_wait(barrier, expected)

    def copy_to(src, dst, send_sem, recv_sem, peer):
        return pltpu.make_async_remote_copy(
            src_ref=src, dst_ref=dst, send_sem=send_sem, recv_sem=recv_sem, device_id=peer, device_id_type=MESH
        )

    mine, group = rows.at[place, sub], rows.at[place]
    sub_copies = [copy_to(mine, mine, sub_send.at[o], sub_recv.at[o], peer) for o, peer in enumerate(sub_ids)]
    curve_copies = [
        copy_to(group, all_rows.at[place], curve_send.at[o], curve_recv.at[o], peer)
        for o, peer in enumerate(curve_ids)
    ]
    box_ends = [(to_right, from_left), (to_left, from_right), (to_second, from_second)]
    box_copies = []
    side_copies = []
    for k, (step, sends, gets) in enumerate(chain):
        peer = device(jnp.clip(me + step, 0, total - 1))
        box_copies.append(copy_to(*box_ends[k], box_send.at[k], box_recv.at[k], peer))
        side_copies.append(copy_to(mine, side.at[k], side_send.at[k], side_recv.at[k], peer))
    for copy in sub_copies:
        copy.start()
    for k, (step, sends, gets) in enumerate(chain):
        @pl.when(sends)
        def _(k=k):
            side_copies[k].start()
            box_copies[k].start()

    for load in loads[3:]:
        load.wait()
    for f in range(fields):
        taps = step_taps(courant[f])
        both = []
        for s in range(11):
            terms = [taps[m] * taps[s - m] for m in range(6) if 0 <= s - m < 6]
            both.append(functools.reduce(lambda a, b: a + b, terms))
        mat = both[0] * joined[0:fine, :]
        for s in range(1, 11):
            mat = mat + both[s] * joined[s : s + fine, :]
        mats[f, 1] = split_pair(mat)
        one = taps[0] * alone[0:fine, :]
        for s in range(1, 6):
            one = one + taps[s] * alone[s : s + fine, :]
        first_step[0:8, :] = jnp.broadcast_to(one[0:1, :], (8, 128))
        first_step[8 : 8 + fine, :] = one
        first_step[8 + fine : 16 + fine, :] = jnp.broadcast_to(one[fine - 1 : fine, :], (8, 128))
        two = taps[0] * first_step[5 : 5 + fine, :]
        for s in range(1, 6):
            two = two + taps[s] * first_step[5 + s : 5 + s + fine, :]
        mats[f, 0] = split_pair(two)

    top = lax.broadcasted_iota(jnp.int32, (8, 256), 0) < 4
    first_lane = lax.broadcasted_iota(jnp.int32, (fine, 128), 1)

    def across(slot, at, left, own, right, mat):
        data = jnp.concatenate([jnp.where(top, right, left), own], axis=0)
        rest = data - data.astype(jnp.bfloat16).astype(jnp.float32)
        stacked = jnp.concatenate([data, rest], axis=0).astype(jnp.bfloat16)
        stacked = jnp.concatenate([stacked, stacked], axis=0)
        moved = jnp.dot(mat[:, 0:96], stacked, preferred_element_type=jnp.float32)
        a, b = moved[:, 0:128], moved[:, 128:256]
        count = mat.shape[0]
        pick = first_lane[0:count]
        for n, part in enumerate([a, jnp.where(pick < 32, b, a), jnp.where(pick < 96, b, a), b]):
            high = part.astype(jnp.bfloat16)
            windows[slot, n, at : at + count, 0:128] = high
            windows[slot, n, at : at + count, 128:256] = (part - high.astype(jnp.float32)).astype(jnp.bfloat16)

    def spread(slot, f, targets):
        count = sum(n for _, _, n in targets)
        for n in range(4):
            plane = jnp.dot(windows[slot, n, 0:count], tables[n], preferred_element_type=jnp.float32)
            at = 0
            for k, start, size in targets:
                cand[k, f, start : start + size, 256 * n : 256 * n + 256] = plane[at : at + size]
                at += size

    def next_to(a, b):
        return jnp.where(box_x[a] + 1 == box_x[b], 1, 0)

    own = []
    for r in range(boxes):
        before, after = rank_box[max(r - 1, 0)], rank_box[min(r + 1, boxes - 1)]
        left_on = next_to(before, rank_box[r]) if r else jnp.int32(0)
        right_on = jnp.where(r + 1 < live, next_to(rank_box[r], after), 0) if r + 1 < boxes else jnp.int32(0)
        own.append((2 + r, before, rank_box[r], after, left_on, right_on))
    own.append((12, tail_box[1], tail_box[2], tail_box[2], next_to(tail_box[1], tail_box[2]), jnp.int32(0)))

    def inner_x(f):
        for i, (_, before, box, after, left_on, right_on) in enumerate(own):
            mat = jnp.concatenate([mats[f, left_on, 0:16, :], mats[f, right_on, 16:32, :]], axis=0)
            across(f % 2, 32 * i, held[before, f, 8:16, :], held[box, f], held[after, f, 0:8, :], mat)

    def inner_yz(f):
        spread(f % 2, f, [(entry[0], 0, 32) for entry in own])

    early = fields // 2
    inner_x(0)
    for f in range(early):
        if f + 1 < early:
            inner_x(f + 1)
        inner_yz(f)

    for copy in sub_copies:
        copy.wait_recv()
    for copy in curve_copies:
        copy.start()
    keep = pltpu.make_async_copy(group, all_rows.at[place], out_sem.at[0])
    keep.start()

    inner_x(early)
    for f in range(early, fields):
        if f + 1 < fields:
            inner_x(f + 1)
        inner_yz(f)
    cand[13] = jnp.zeros(cand.shape[1:], jnp.float32)

    for k, (step, sends, gets) in enumerate(chain):
        @pl.when(gets)
        def _(k=k):
            side_copies[k].wait_recv()
            box_copies[k].wait_recv()
    right_row, left_row, second_row = side[1], side[0], side[2]
    left_x = [jnp.sum(jnp.where(lane == 1 + k, left_row, 0)) for k in range(3)]
    short = jnp.sum(jnp.where(lane == 7, left_row, 0)) < 3
    left_x[0] = jnp.where(short, jnp.sum(jnp.where(lane == 3, second_row, 0)), left_x[0])
    right_x = [jnp.sum(jnp.where(lane == 4 + k, right_row, 0)) for k in range(3)]

    def joins(a, b, there):
        return jnp.where(there & (a + 1 == b), 1, 0)

    low, high = me > 0, me < total - 1
    low_rim = joins(left_x[0], left_x[1], low)
    low_pair = joins(left_x[1], left_x[2], low)
    low_own = joins(left_x[2], box_x[head_box[0]], low)
    high_own = joins(box_x[tail_box[2]], right_x[0], high)
    high_pair = joins(right_x[0], right_x[1], high)
    high_rim = joins(right_x[1], right_x[2], high)

    def outer_x(f):
        slot, at, rim = f % 2, 32 * f, 32 * fields + 8 * (f // 2)
        left_rim = jnp.where(short, from_second[rim - 32 * fields : rim - 32 * fields + 8, :], from_left[rim : rim + 8, :])
        right_rim = from_right[rim : rim + 8, :]
        if f % 2 == 0:
            left_rim = pltpu.roll(left_rim, 4, 0)
        else:
            right_rim = pltpu.roll(right_rim, 4, 0)
        zero = jnp.zeros((8, 256), jnp.float32)
        head, tail = held[head_box[0], f, 0:8, :], held[tail_box[2], f, 8:16, :]

        def both(a, b):
            return jnp.concatenate([mats[f, a, 0:16, :], mats[f, b, 16:32, :]], axis=0)

        across(slot, 0, left_rim, from_left[at : at + 16, :], from_left[at + 16 : at + 24, :], both(low_rim, low_pair))
        across(slot, 32, from_left[at + 8 : at + 16, :], from_left[at + 16 : at + 32, :], head, both(low_pair, low_own))
        edge = jnp.where(low_own == 1, from_left[at + 24 : at + 32, :], zero)
        across(slot, 64, edge, held[head_box[0], f], held[head_box[0], f, 8:16, :], mats[f, low_own, 0:16, :])
        edge = jnp.where(high_own == 1, from_right[at : at + 8, :], zero)
        across(slot, 80, held[tail_box[2], f, 0:8, :], held[tail_box[2], f], edge, mats[f, high_own, 16:32, :])
        across(slot, 96, tail, from_right[at : at + 16, :], from_right[at + 16 : at + 24, :], both(high_own, high_pair))
        across(slot, 128, from_right[at + 8 : at + 16, :], from_right[at + 16 : at + 32, :], right_rim, both(high_pair, high_rim))

    def outer_yz(f):
        spread(f % 2, f, [(0, 0, 32), (1, 0, 32), (2, 0, 16), (12, 16, 16), (10, 0, 32), (11, 0, 32)])

    outer_x(0)
    for f in range(fields):
        if f + 1 < fields:
            outer_x(f + 1)
        outer_yz(f)

    keep.wait()
    for copy in curve_copies:
        copy.wait_recv()
    for copy in sub_copies + curve_copies:
        copy.wait_send()
    for k, (step, sends, gets) in enumerate(chain):
        @pl.when(sends)
        def _(k=k):
            side_copies[k].wait_send()
            box_copies[k].wait_send()


def settle(n_curve, n_sub, all_rows, cand, out, sems):
    boxes = out.shape[0]
    n_half = n_curve // 2
    curve, sub = lax.axis_index("curve"), lax.axis_index("sub")
    shape = all_rows.shape
    order = lax.broadcasted_iota(jnp.int32, shape, 0)
    lanes = lax.broadcasted_iota(jnp.int32, shape, 1)
    spot = (curve % n_half) * n_sub + sub
    rows = all_rows[...]
    below = jnp.where((lanes == 0) & (order < spot), rows, 0)
    above = jnp.where((lanes == 0) & (order >= spot), rows, 0)
    offset = jnp.sum(jnp.where(curve < n_half, below, -above))
    change = jnp.sum(jnp.where((lanes == 0) & (order == spot), rows, 0))
    live = jnp.sum(jnp.where((lanes == 7) & (order == spot), rows, 0))
    copies = []
    for j in range(boxes):
        rank = offset + j
        pick = jnp.where(rank < live - 1, 2 + rank, jnp.where(rank == live - 1, 12, 10 + rank - live))
        pick = jnp.clip(jnp.where(j < live + change, pick, 13), 0, 13)
        copy = pltpu.make_async_copy(cand.at[pick], out.at[j], sems.at[j])
        copy.start()
        copies.append(copy)
    for copy in copies:
        copy.wait()


def local(n_curve, n_sub, coarse, tags, box_x, counts, courant):
    boxes, fields, half, plane = coarse.shape
    fine = 2 * half
    joined, alone = x_tables(half)
    tables = jnp.asarray(plane_tables(half), jnp.bfloat16)
    vmem = pl.BlockSpec(memory_space=pltpu.VMEM)
    anywhere = pl.BlockSpec(memory_space=pl.ANY)
    stay = pl.BlockSpec(memory_space=pltpu.HBM)
    packed = 36 * fields
    dma = pltpu.SemaphoreType.DMA
    n_half = n_curve // 2
    edge = pltpu.VMEM((packed, plane), jnp.float32)
    rim = pltpu.VMEM((4 * fields, plane), jnp.float32)
    inputs = (tags, box_x, courant, coarse, jnp.asarray(joined), jnp.asarray(alone), tables)
    all_rows, cand = pl.pallas_call(
        functools.partial(exchange, n_curve, n_sub),
        out_shape=(
            jax.ShapeDtypeStruct((n_half, n_sub, 1, 128), jnp.int32),
            jax.ShapeDtypeStruct((boxes + 6, fields, fine, 4 * plane), jnp.float32),
        ),
        in_specs=[stay] * 7 + [pl.BlockSpec(memory_space=pltpu.SMEM)],
        out_specs=(vmem, vmem),
        scratch_shapes=[
            pltpu.SMEM((boxes,), jnp.int32),
            pltpu.SMEM((boxes,), jnp.int32),
            pltpu.SMEM((fields,), jnp.float32),
            pltpu.VMEM((48, 128), jnp.float32),
            pltpu.VMEM((40, 128), jnp.float32),
            pltpu.VMEM(tables.shape, jnp.bfloat16),
            pltpu.VMEM((fields, 2, fine, 128), jnp.bfloat16),
            pltpu.VMEM((2, 4, (boxes + 1) * fine, plane), jnp.bfloat16),
            pltpu.VMEM(coarse.shape, jnp.float32),
            edge, edge, rim,
            edge, edge, rim,
            pltpu.VMEM((n_half, n_sub, 1, 128), jnp.int32),
            pltpu.VMEM((3, 1, 128), jnp.int32),
            pltpu.VMEM((48, 128), jnp.float32),
            dma((7,)),
            dma((1,)),
            dma((3,)),
            dma((3,)),
            dma((3,)),
            dma((3,)),
            dma((n_sub - 1,)),
            dma((n_sub - 1,)),
            dma((n_half - 1,)),
            dma((n_half - 1,)),
        ],
        compiler_params=pltpu.CompilerParams(collective_id=0, has_side_effects=True, vmem_limit_bytes=24 * 2**20),
        name="exchange",
    )(*[pltpu.with_memory_space_constraint(a, pltpu.HBM) for a in inputs], counts)
    return pl.pallas_call(
        functools.partial(settle, n_curve, n_sub),
        out_shape=jax.ShapeDtypeStruct((boxes, fields, fine, 4 * plane), jnp.float32),
        in_specs=[vmem, vmem],
        out_specs=anywhere,
        scratch_shapes=[dma((boxes,))],
        compiler_params=pltpu.CompilerParams(vmem_limit_bytes=16 * 2**20),
        name="settle",
    )(all_rows.reshape(n_half * n_sub, 128), cand)


def solution(mesh):
    both = ("curve", "sub")
    in_specs = (P(both, None, None, None), P(both), P(both), P(both), P())
    return jax.shard_map(
        functools.partial(local, mesh.shape["curve"], mesh.shape["sub"]),
        mesh=mesh,
        in_specs=in_specs,
        out_specs=P(both, None, None, None),
        check_vma=False,
    )
```

time: 20.4 us -> 17.3 us (0.85)
  Pallas kernels: 19.5 us -> 16.5 us
    pallas_call x1, Pallas kernels: 5.81 us -> 2.91 us  [local(): pl.pallas_call(functools.partial(settle, n_curve, n_sub), out_shape=jax.S...]
where the time goes in v3:
time: 17.3 us; the launch traced here: 17.2 us
  Pallas kernels  16.5 us (95%)
  between operations  0.66 us (4%)
    pallas_call x1, Pallas kernels, local(): pl.pallas_call(functools.partial(exchange, n_curve, n_sub), out_shape=(ja...  13.6 us
    pallas_call x1, Pallas kernels, local(): pl.pallas_call(functools.partial(settle, n_curve, n_sub), out_shape=jax.S...  2.91 us

profile of v3, /device:TPU:1, one launch (start us, length us, event | category | flops | bytes accessed | tf_op | source)
XLA Modules:
  0.0 17.2 jit_solution(1985948111298247407)
XLA Ops:
  0.7 13.6 %exchange.1 = (s32[8,8,1,128]{3,2,1,0:T(1,128)S(1)}, f32[14,6,32,1024]{3,2,1,0:T(8,128)S(1)}) custom-call(s32[8]{0:T(128)} %tags_in.1, s32[8]{0:T(128)} %box_x_in.1, f32[6]{0:T(128)} %courant_in.1, f32[8,6,16,256]{3,2,1,0:T(8,128)} %coarse.1, f32[48,128]{1,0:T(8,128)} %constant.7.clone.joined_in, f32[40,128]{1,0:T(8,128)} %constant.8.clone.alone_in, ...), custom_call_target="tpu_custom_call" | custom-call | tf_op jit(solution)/shard_map/exchange/pallas_call | solution.py:398
  14.3 2.9 %settle.1 = f32[8,6,32,1024]{3,2,1,0:T(8,128)} custom-call(s32[64,128]{1,0:T(8,128)S(1)} %bitcast.1, f32[14,6,32,1024]{3,2,1,0:T(8,128)S(1)} %get-tuple-element.8.cand), custom_call_target="tpu_custom_call" | custom-call | tf_op jit(solution)/shard_map/settle/pallas_call | solution.py:435

commit v4 on v3

--- a/solution.py
+++ b/solution.py
@@ -127,14 +127,20 @@
     ]
     for load in loads:
         load.start()
-    for peer in curve_ids + sub_ids:
+    goes = [jnp.where(upper == 0, place + o < n_half, place + o >= n_half) for o in range(1, n_half)]
+    comes = [jnp.where(upper == 0, place - o >= 0, place - o < 0) for o in range(1, n_half)]
+    for o in range(1, n_half):
+        @pl.when(comes[o - 1])
+        def _(o=o):
+            signal((upper * n_half + (place - o + n_half) % n_half, sub))
+    for peer in sub_ids:
         signal(peer)
-    expected = jnp.int32(len(curve_ids) + len(sub_ids))
-    for step, sends, gets in chain + [(-2, me > 1, me < total - 2)]:
-        @pl.when(sends)
+    expected = jnp.int32(len(sub_ids)) + jnp.where(upper == 0, n_half - 1 - place, place)
+    for step, sends, gets in chain:
+        @pl.when(gets)
         def _(step=step):
-            signal(device(me + step))
-        expected = expected + jnp.where(gets, 1, 0)
+            signal(device(me - step))
+        expected = expected + jnp.where(sends, 1, 0)
 
     for load in loads[1:3]:
         load.wait()
@@ -277,8 +283,8 @@
 
     for copy in sub_copies:
         copy.wait_recv()
-    for copy in curve_copies:
-        copy.start()
+    for o, copy in enumerate(curve_copies):
+        pl.when(goes[o])(copy.start)
     keep = pltpu.make_async_copy(group, all_rows.at[place], out_sem.at[0])
     keep.start()
 
@@ -344,10 +350,12 @@
         outer_yz(f)
 
     keep.wait()
-    for copy in curve_copies:
-        copy.wait_recv()
-    for copy in sub_copies + curve_copies:
+    for o, copy in enumerate(curve_copies):
+        pl.when(comes[o])(copy.wait_recv)
+    for copy in sub_copies:
         copy.wait_send()
+    for o, copy in enumerate(curve_copies):
+        pl.when(goes[o])(copy.wait_send)
     for k, (step, sends, gets) in enumerate(chain):
         @pl.when(sends)
         def _(k=k):

time: 17.3 us -> 16.5 us (0.954)
  Pallas kernels: 16.5 us -> 15.8 us
    pallas_call x1, Pallas kernels: 13.6 us -> 12.8 us  [local(): pl.pallas_call(functools.partial(exchange, n_curve, n_sub), out_shape=(ja...]
where the time goes in v4:
time: 16.5 us; the launch traced here: 16.4 us
  Pallas kernels  15.8 us (96%)
  between operations  0.66 us (4%)
    pallas_call x1, Pallas kernels, local(): pl.pallas_call(functools.partial(exchange, n_curve, n_sub), out_shape=(ja...  12.8 us
    pallas_call x1, Pallas kernels, local(): pl.pallas_call(functools.partial(settle, n_curve, n_sub), out_shape=jax.S...  2.91 us

profile of v4, /device:TPU:1, one launch (start us, length us, event | category | flops | bytes accessed | tf_op | source)
XLA Modules:
  0.0 16.4 jit_solution(3024831762840745026)
XLA Ops:
  0.7 12.8 %exchange.1 = (s32[8,8,1,128]{3,2,1,0:T(1,128)S(1)}, f32[14,6,32,1024]{3,2,1,0:T(8,128)S(1)}) custom-call(s32[8]{0:T(128)} %tags_in.1, s32[8]{0:T(128)} %box_x_in.1, f32[6]{0:T(128)} %courant_in.1, f32[8,6,16,256]{3,2,1,0:T(8,128)} %coarse.1, f32[48,128]{1,0:T(8,128)} %constant.7.clone.joined_in, f32[40,128]{1,0:T(8,128)} %constant.8.clone.alone_in, ...), custom_call_target="tpu_custom_call" | custom-call | tf_op jit(solution)/shard_map/exchange/pallas_call | solution.py:406
  13.5 2.9 %settle.1 = f32[8,6,32,1024]{3,2,1,0:T(8,128)} custom-call(s32[64,128]{1,0:T(8,128)S(1)} %bitcast.1, f32[14,6,32,1024]{3,2,1,0:T(8,128)S(1)} %get-tuple-element.8.cand), custom_call_target="tpu_custom_call" | custom-call | tf_op jit(solution)/shard_map/settle/pallas_call | solution.py:443

commit v5 on v4

--- a/solution.py
+++ b/solution.py
@@ -91,7 +91,7 @@
     tags_in, box_x_in, courant_in, coarse, joined_in, alone_in, tables_in, counts,
     all_rows, cand,
     tags, box_x, courant, joined, alone, tables, mats, windows,
-    held, to_right, to_left, to_second, from_left, from_right, from_second, rows, side, first_step,
+    held, to_right, to_left, to_second, from_left, from_right, from_second, rows, beside, first_step,
     load_sem, out_sem, box_send, box_recv, side_send, side_recv, sub_send, sub_recv, curve_send, curve_recv,
 ):
     boxes = coarse.shape[0]
@@ -178,34 +178,6 @@
         to_left[at : at + 16, :] = held[head_box[0], f]
         to_left[at + 16 : at + 32, :] = held[head_box[1], f]
         to_left[rim + low : rim + low + 4, :] = held[head_box[2], f, 0:4, :]
-    pl.semaphore_wait(barrier, expected)
-
-    def copy_to(src, dst, send_sem, recv_sem, peer):
-        return pltpu.make_async_remote_copy(
-            src_ref=src, dst_ref=dst, send_sem=send_sem, recv_sem=recv_sem, device_id=peer, device_id_type=MESH
-        )
-
-    mine, group = rows.at[place, sub], rows.at[place]
-    sub_copies = [copy_to(mine, mine, sub_send.at[o], sub_recv.at[o], peer) for o, peer in enumerate(sub_ids)]
-    curve_copies = [
-        copy_to(group, all_rows.at[place], curve_send.at[o], curve_recv.at[o], peer)
-        for o, peer in enumerate(curve_ids)
-    ]
-    box_ends = [(to_right, from_left), (to_left, from_right), (to_second, from_second)]
-    box_copies = []
-    side_copies = []
-    for k, (step, sends, gets) in enumerate(chain):
-        peer = device(jnp.clip(me + step, 0, total - 1))
-        box_copies.append(copy_to(*box_ends[k], box_send.at[k], box_recv.at[k], peer))
-        side_copies.append(copy_to(mine, side.at[k], side_send.at[k], side_recv.at[k], peer))
-    for copy in sub_copies:
-        copy.start()
-    for k, (step, sends, gets) in enumerate(chain):
-        @pl.when(sends)
-        def _(k=k):
-            side_copies[k].start()
-            box_copies[k].start()
-
     for load in loads[3:]:
         load.wait()
     for f in range(fields):
@@ -266,20 +238,55 @@
         own.append((2 + r, before, rank_box[r], after, left_on, right_on))
     own.append((12, tail_box[1], tail_box[2], tail_box[2], next_to(tail_box[1], tail_box[2]), jnp.int32(0)))
 
-    def inner_x(f):
-        for i, (_, before, box, after, left_on, right_on) in enumerate(own):
-            mat = jnp.concatenate([mats[f, left_on, 0:16, :], mats[f, right_on, 16:32, :]], axis=0)
-            across(f % 2, 32 * i, held[before, f, 8:16, :], held[box, f], held[after, f, 0:8, :], mat)
-
-    def inner_yz(f):
-        spread(f % 2, f, [(entry[0], 0, 32) for entry in own])
-
-    early = fields // 2
-    inner_x(0)
-    for f in range(early):
-        if f + 1 < early:
-            inner_x(f + 1)
-        inner_yz(f)
+    def inner(h, carry):
+        count = fields // 2
+
+        def inner_x(k):
+            f = count * h + k
+            for i, (_, before, box, after, left_on, right_on) in enumerate(own):
+                mat = jnp.concatenate([mats[f, left_on, 0:16, :], mats[f, right_on, 16:32, :]], axis=0)
+                across(k % 2, 32 * i, held[before, f, 8:16, :], held[box, f], held[after, f, 0:8, :], mat)
+
+        inner_x(0)
+        for k in range(count):
+            if k + 1 < count:
+                inner_x(k + 1)
+            spread(k % 2, count * h + k, [(entry[0], 0, 32) for entry in own])
+        return carry
+
+    row_y, chip_x = curve % 4, sub // 2
+    done = jnp.where(chip_x + row_y == 0, 2, jnp.where((row_y == 0) | (chip_x == 0), 1, 0))
+    then = jnp.minimum(done + 1, 2)
+    lax.fori_loop(0, done, inner, 0)
+    pl.semaphore_wait(barrier, expected)
+
+    def copy_to(src, dst, send_sem, recv_sem, peer):
+        return pltpu.make_async_remote_copy(
+            src_ref=src, dst_ref=dst, send_sem=send_sem, recv_sem=recv_sem, device_id=peer, device_id_type=MESH
+        )
+
+    mine, group = rows.at[place, sub], rows.at[place]
+    sub_copies = [copy_to(mine, mine, sub_send.at[o], sub_recv.at[o], peer) for o, peer in enumerate(sub_ids)]
+    curve_copies = [
+        copy_to(group, all_rows.at[place], curve_send.at[o], curve_recv.at[o], peer)
+        for o, peer in enumerate(curve_ids)
+    ]
+    box_ends = [(to_right, from_left), (to_left, from_right), (to_second, from_second)]
+    box_copies = []
+    side_copies = []
+    for k, (step, sends, gets) in enumerate(chain):
+        peer = device(jnp.clip(me + step, 0, total - 1))
+        box_copies.append(copy_to(*box_ends[k], box_send.at[k], box_recv.at[k], peer))
+        side_copies.append(copy_to(mine, beside.at[k], side_send.at[k], side_recv.at[k], peer))
+    for copy in sub_copies:
+        copy.start()
+    for k, (step, sends, gets) in enumerate(chain):
+        @pl.when(sends)
+        def _(k=k):
+            side_copies[k].start()
+            box_copies[k].start()
+
+    lax.fori_loop(done, then, inner, 0)
 
     for copy in sub_copies:
         copy.wait_recv()
@@ -288,66 +295,108 @@
     keep = pltpu.make_async_copy(group, all_rows.at[place], out_sem.at[0])
     keep.start()
 
-    inner_x(early)
-    for f in range(early, fields):
-        if f + 1 < fields:
-            inner_x(f + 1)
-        inner_yz(f)
+    lax.fori_loop(then, 2, inner, 0)
     cand[13] = jnp.zeros(cand.shape[1:], jnp.float32)
 
-    for k, (step, sends, gets) in enumerate(chain):
-        @pl.when(gets)
-        def _(k=k):
-            side_copies[k].wait_recv()
-            box_copies[k].wait_recv()
-    right_row, left_row, second_row = side[1], side[0], side[2]
-    left_x = [jnp.sum(jnp.where(lane == 1 + k, left_row, 0)) for k in range(3)]
-    short = jnp.sum(jnp.where(lane == 7, left_row, 0)) < 3
-    left_x[0] = jnp.where(short, jnp.sum(jnp.where(lane == 3, second_row, 0)), left_x[0])
-    right_x = [jnp.sum(jnp.where(lane == 4 + k, right_row, 0)) for k in range(3)]
+    def arrive(which):
+        for k in which:
+            @pl.when(chain[k][2])
+            def _(k=k):
+                side_copies[k].wait_recv()
+                box_copies[k].wait_recv()
 
     def joins(a, b, there):
         return jnp.where(there & (a + 1 == b), 1, 0)
 
-    low, high = me > 0, me < total - 1
-    low_rim = joins(left_x[0], left_x[1], low)
-    low_pair = joins(left_x[1], left_x[2], low)
-    low_own = joins(left_x[2], box_x[head_box[0]], low)
-    high_own = joins(box_x[tail_box[2]], right_x[0], high)
-    high_pair = joins(right_x[0], right_x[1], high)
-    high_rim = joins(right_x[1], right_x[2], high)
-
-    def outer_x(f):
-        slot, at, rim = f % 2, 32 * f, 32 * fields + 8 * (f // 2)
+    def pair(f, a, b):
+        return jnp.concatenate([mats[f, a, 0:16, :], mats[f, b, 16:32, :]], axis=0)
+
+    zero = jnp.zeros((8, 256), jnp.float32)
+
+    def in_turn(x_part, targets):
+        x_part(0)
+        for f in range(fields):
+            if f + 1 < fields:
+                x_part(f + 1)
+            spread(f % 2, f, targets)
+
+    def left_joins(whole):
+        left_row = beside[0]
+        low = me > 0
+        left_x = [jnp.sum(jnp.where(lane == 1 + k, left_row, 0)) for k in range(3)]
+        low_pair = joins(left_x[1], left_x[2], low)
+        low_own = joins(left_x[2], box_x[head_box[0]], low)
+        if not whole:
+            return low_pair, low_own
+        short = jnp.sum(jnp.where(lane == 7, left_row, 0)) < 3
+        third = jnp.where(short, jnp.sum(jnp.where(lane == 3, beside[2], 0)), left_x[0])
+        return low_pair, low_own, short, joins(third, left_x[1], low)
+
+    def far_box(slot, start, f, flags):
+        low_pair, _, short, low_rim = flags
+        at, rim = 32 * f, 32 * fields + 8 * (f // 2)
         left_rim = jnp.where(short, from_second[rim - 32 * fields : rim - 32 * fields + 8, :], from_left[rim : rim + 8, :])
-        right_rim = from_right[rim : rim + 8, :]
         if f % 2 == 0:
             left_rim = pltpu.roll(left_rim, 4, 0)
-        else:
-            right_rim = pltpu.roll(right_rim, 4, 0)
-        zero = jnp.zeros((8, 256), jnp.float32)
-        head, tail = held[head_box[0], f, 0:8, :], held[tail_box[2], f, 8:16, :]
-
-        def both(a, b):
-            return jnp.concatenate([mats[f, a, 0:16, :], mats[f, b, 16:32, :]], axis=0)
-
-        across(slot, 0, left_rim, from_left[at : at + 16, :], from_left[at + 16 : at + 24, :], both(low_rim, low_pair))
-        across(slot, 32, from_left[at + 8 : at + 16, :], from_left[at + 16 : at + 32, :], head, both(low_pair, low_own))
-        edge = jnp.where(low_own == 1, from_left[at + 24 : at + 32, :], zero)
-        across(slot, 64, edge, held[head_box[0], f], held[head_box[0], f, 8:16, :], mats[f, low_own, 0:16, :])
-        edge = jnp.where(high_own == 1, from_right[at : at + 8, :], zero)
-        across(slot, 80, held[tail_box[2], f, 0:8, :], held[tail_box[2], f], edge, mats[f, high_own, 16:32, :])
-        across(slot, 96, tail, from_right[at : at + 16, :], from_right[at + 16 : at + 24, :], both(high_own, high_pair))
-        across(slot, 128, from_right[at + 8 : at + 16, :], from_right[at + 16 : at + 32, :], right_rim, both(high_pair, high_rim))
-
-    def outer_yz(f):
-        spread(f % 2, f, [(0, 0, 32), (1, 0, 32), (2, 0, 16), (12, 16, 16), (10, 0, 32), (11, 0, 32)])
-
-    outer_x(0)
-    for f in range(fields):
-        if f + 1 < fields:
-            outer_x(f + 1)
-        outer_yz(f)
+        across(slot, start, left_rim, from_left[at : at + 16, :], from_left[at + 16 : at + 24, :], pair(f, low_rim, low_pair))
+
+    def left_part(whole):
+        arrive((0, 2) if whole else (0,))
+        flags = left_joins(whole)
+        low_pair, low_own = flags[:2]
+
+        def x_part(f):
+            slot, at = f % 2, 32 * f
+            head = held[head_box[0], f, 0:8, :]
+            across(slot, 0, from_left[at + 8 : at + 16, :], from_left[at + 16 : at + 32, :], head, pair(f, low_pair, low_own))
+            edge = jnp.where(low_own == 1, from_left[at + 24 : at + 32, :], zero)
+            across(slot, 32, edge, held[head_box[0], f], held[head_box[0], f, 8:16, :], mats[f, low_own, 0:16, :])
+            if whole:
+                far_box(slot, 48, f, flags)
+
+        in_turn(x_part, [(1, 0, 32), (2, 0, 16)] + ([(0, 0, 32)] if whole else []))
+
+    def right_part(extra):
+        arrive((1, 2) if extra else (1,))
+        flags = left_joins(True) if extra else None
+        right_row = beside[1]
+        high = me < total - 1
+        right_x = [jnp.sum(jnp.where(lane == 4 + k, right_row, 0)) for k in range(3)]
+        high_own = joins(box_x[tail_box[2]], right_x[0], high)
+        high_pair = joins(right_x[0], right_x[1], high)
+        high_rim = joins(right_x[1], right_x[2], high)
+
+        def x_part(f):
+            slot, at, rim = f % 2, 32 * f, 32 * fields + 8 * (f // 2)
+            right_rim = from_right[rim : rim + 8, :]
+            if f % 2:
+                right_rim = pltpu.roll(right_rim, 4, 0)
+            tail = held[tail_box[2], f, 8:16, :]
+            across(slot, 0, tail, from_right[at : at + 16, :], from_right[at + 16 : at + 24, :], pair(f, high_own, high_pair))
+            across(slot, 32, from_right[at + 8 : at + 16, :], from_right[at + 16 : at + 32, :], right_rim, pair(f, high_pair, high_rim))
+            edge = jnp.where(high_own == 1, from_right[at : at + 8, :], zero)
+            across(slot, 64, held[tail_box[2], f, 0:8, :], held[tail_box[2], f], edge, mats[f, high_own, 16:32, :])
+            if extra:
+                far_box(slot, 80, f, flags)
+
+        in_turn(x_part, [(10, 0, 32), (11, 0, 32), (12, 16, 16)] + ([(0, 0, 32)] if extra else []))
+
+    even, turn = sub % 2 == 0, (sub == 1) & (me > 1)
+
+    @pl.when(even)
+    def _():
+        right_part(False)
+        left_part(True)
+
+    @pl.when(turn)
+    def _():
+        left_part(False)
+        right_part(True)
+
+    @pl.when(jnp.logical_not(even | turn))
+    def _():
+        left_part(True)
+        right_part(False)
 
     keep.wait()
     for o, copy in enumerate(curve_copies):

time: 16.5 us -> 16.4 us (level)
  Pallas kernels: 15.8 us -> 15.6 us
where the time goes in v5:
time: 16.4 us; the launch traced here: 16.3 us
  Pallas kernels  15.6 us (95%)
  between operations  0.66 us (4%)
    pallas_call x1, Pallas kernels, local(): pl.pallas_call(functools.partial(exchange, n_curve, n_sub), out_shape=(ja...  12.7 us
    pallas_call x1, Pallas kernels, local(): pl.pallas_call(functools.partial(settle, n_curve, n_sub), out_shape=jax.S...  2.91 us

profile of v5, /device:TPU:1, one launch (start us, length us, event | category | flops | bytes accessed | tf_op | source)
XLA Modules:
  0.0 16.3 jit_solution(9500398177410234490)
XLA Ops:
  0.7 12.7 %exchange.1 = (s32[8,8,1,128]{3,2,1,0:T(1,128)S(1)}, f32[14,6,32,1024]{3,2,1,0:T(8,128)S(1)}) custom-call(s32[8]{0:T(128)} %tags_in.1, s32[8]{0:T(128)} %box_x_in.1, f32[6]{0:T(128)} %courant_in.1, f32[8,6,16,256]{3,2,1,0:T(8,128)} %coarse.1, f32[48,128]{1,0:T(8,128)} %constant.7.clone.joined_in, f32[40,128]{1,0:T(8,128)} %constant.8.clone.alone_in, ...), custom_call_target="tpu_custom_call" | custom-call | tf_op jit(solution)/shard_map/exchange/pallas_call | solution.py:455
  13.4 2.9 %settle.1 = f32[8,6,32,1024]{3,2,1,0:T(8,128)} custom-call(s32[64,128]{1,0:T(8,128)S(1)} %bitcast.1, f32[14,6,32,1024]{3,2,1,0:T(8,128)S(1)} %get-tuple-element.8.cand), custom_call_target="tpu_custom_call" | custom-call | tf_op jit(solution)/shard_map/settle/pallas_call | solution.py:492
